TPU v7x, 512 devices: a whole 4x4x16 slice. The times are simulated.
512 devices in a mesh: tile: 16 (over y, z_lo), sub: 32 (over z_hi, x, core).
Axes of the slice: x: 4, y: 4, z: 16 (z_hi: 4, z_lo: 4; z = z_hi * 4 + z_lo), core: 2. Of those that a mesh axis runs over, the one named last changes fastest.
Arguments:
- seeds: float32 [16, 6, 64, 256, 128], P('tile', None, 'sub'), may hold values from -6 to 6
- material: int32 [16, 64, 256, 128], P('tile', 'sub'), may hold values from 0 to 3
- decay: float32 [4], replicated, may hold values from 0.5 to 1
- coupling: float32 [4], replicated, may hold values from 0.1 to 0.6
Outputs:
- gradient: float32 [16, 6, 64, 256, 128], P('tile', None, 'sub')
All inputs are finite; a program needn't handle non-finite values.
Results may differ from a plain program's by a relative error of at most 0.0003.
Values sent between devices are 32-bit elements; how exact they have to be, the bound alone decides.
A program may use at most 64 MiB of HBM per device.

v0:
```python
import math

import jax
import jax.numpy as jnp
from jax import lax
from jax.sharding import PartitionSpec as P

BAND = 32
STEPS = 2


magnetic_coeff = 0.5


def passed_along(block, axis, distance):
    devices = range(lax.axis_size(axis))
    route = [(i - distance, i) for i in devices if i - distance in devices]
    return lax.ppermute(block, axis, route)


def from_behind(value, axis, steps):
    count = lax.axis_size(axis)
    pairs = [(source, (source + steps) % count) for source in range(count)]
    return lax.ppermute(value, axis, pairs)


def lookup_table(material, table):
    labels = jnp.arange(table.shape[0], dtype=jnp.int32)[:, None, None, None]
    return jnp.sum(jnp.where(material[None] == labels, table[:, None, None, None], 0.0), axis=0)


def plus_diff(values, axis_pos):
    width = values.shape[axis_pos]
    later = lax.slice_in_dim(values, 1, width, axis=axis_pos)
    padding = [(0, 0)] * values.ndim
    padding[axis_pos] = (0, 1)
    return jnp.pad(later, padding) - values


def minus_diff(values, axis_pos):
    width = values.shape[axis_pos]
    earlier = lax.slice_in_dim(values, 0, width - 1, axis=axis_pos)
    padding = [(0, 0)] * values.ndim
    padding[axis_pos] = (1, 0)
    return values - jnp.pad(earlier, padding)


def plus_depth(values, after_plane):
    return jnp.concatenate([values[1:], after_plane[None]], axis=0) - values


def minus_depth(values, before_plane):
    return values - jnp.concatenate([before_plane[None], values[:-1]], axis=0)


def curl_forward(fields, after):
    curl_x = plus_diff(fields[2], 2) - plus_depth(fields[1], after[1])
    curl_y = plus_depth(fields[0], after[0]) - plus_diff(fields[2], 1)
    curl_z = plus_diff(fields[1], 1) - plus_diff(fields[0], 2)
    return jnp.stack([curl_x, curl_y, curl_z])


def curl_backward(fields, before):
    curl_x = minus_diff(fields[2], 2) - minus_depth(fields[1], before[1])
    curl_y = minus_depth(fields[0], before[0]) - minus_diff(fields[2], 1)
    curl_z = minus_diff(fields[1], 1) - minus_diff(fields[0], 2)
    return jnp.stack([curl_x, curl_y, curl_z])


def ramp(count):
    position = jnp.arange(count).astype(jnp.float32) + 0.5
    low_part = position / BAND
    high_part = (count - position) / BAND
    return jnp.where(position < BAND, low_part, jnp.where(position > count - BAND, high_part, 1.0))


def send_back(planes):
    return passed_along(planes, "sub", 1)


def on_device(seeds, material, decay, coupling):
    seed_tile = seeds[0]
    material_tile = material[0]
    depth, size_x, size_y = (seed_tile.shape[1], seed_tile.shape[2], seed_tile.shape[3])
    decay_map = lookup_table(material_tile, decay)
    coupling_map = lookup_table(material_tile, coupling)
    field_e = seed_tile[:3]
    field_h = seed_tile[3:]
    for turn_index in range(STEPS):
        scaled = coupling_map * field_e
        after = passed_along(jnp.stack([scaled[0, 0], scaled[1, 0]]), "sub", -1)
        field_h = field_h + curl_forward(scaled, after)
        before = send_back(jnp.stack([field_h[0, -1], field_h[1, -1]]))
        field_e = decay_map * field_e - magnetic_coeff * curl_backward(field_h, before)
    adjoint = jnp.concatenate([field_e, field_h], axis=0)
    side = math.isqrt(lax.axis_size("tile"))
    weight = ramp(size_x)[:, None] * ramp(size_y)[None, :]
    weighted = adjoint * weight
    prev_band = from_behind(weighted[:, :, size_x - BAND :, :], "tile", 1)
    next_band = from_behind(weighted[:, :, :BAND, :], "tile", -1)
    combined = weighted.at[:, :, :BAND, :].add(prev_band)
    combined = combined.at[:, :, size_x - BAND :, :].add(next_band)
    flat_rows = size_x * BAND // 128
    top_slab = combined[..., size_y - BAND :].reshape(6, depth, flat_rows, 128)
    bottom_slab = combined[..., :BAND].reshape(6, depth, flat_rows, 128)
    from_below = from_behind(top_slab, "tile", side).reshape(6, depth, size_x, BAND)
    from_above = from_behind(bottom_slab, "tile", -side).reshape(6, depth, size_x, BAND)
    result = combined.at[..., :BAND].add(from_below)
    result = result.at[..., size_y - BAND :].add(from_above)
    return result[None]


def solution(mesh):
    placed = (P("tile", None, "sub", None, None), P("tile", "sub", None, None), P(), P())
    return jax.shard_map(
        on_device,
        mesh=mesh,
        in_specs=placed,
        out_specs=P("tile", None, "sub", None, None),
        check_vma=False,
    )
```

profile of v0, /device:TPU:7, one launch (start us, length us, event | category | flops | bytes accessed | tf_op | source)
XLA Modules:
  0.0 129.4 jit_solution(8687671603784841849)
XLA Ops:
  0.0 1.2 select_reduce_fusion.1
  1.2 1.2 bitcast_multiply_fusion
  2.5 2.6 %collective-permute-start = (f32[2,256,128]{2,1,0:T(8,128)S(1)}, f32[2,256,128]{2,1,0:T(8,128)S(1)}, u32[]{:S(2)}, u32[]{:S(2)}) collective-permute-start(f32[2,256,128]{2,1,0:T(8,128)S(1)} %pad_maximum_fusion), channel_id=1, source_target_pairs={{1,0},{2,1},{3,2},{4,3},{5,4},{6,5},{7,6},{8,7},{9,8},{10,9},{11,1... | collective-permute-start | bytes 786440 | tf_op jit(solution)/shard_map/ppermute | solution.py:18
  5.1 0.1 slice_bitcast_fusion.11
  5.2 0.1 slice.407
  5.3 0.1 slice.418
  5.5 16.2 %collective-permute-done = f32[2,256,128]{2,1,0:T(8,128)S(1)} collective-permute-done((f32[2,256,128]{2,1,0:T(8,128)S(1)}, f32[2,256,128]{2,1,0:T(8,128)S(1)}, u32[]{:S(2)}, u32[]{:S(2)}) %collective-permute-start) | collective-permute-done | bytes 262176 | tf_op jit(solution)/shard_map/ppermute | solution.py:18
  21.7 0.0 copy-start.1
  21.7 0.1 fusion.4
  21.8 1.3 copy-done.1
  23.1 0.1 maximum_add_fusion
  23.3 1.9 %collective-permute-start.1 = (f32[2,256,128]{2,1,0:T(8,128)S(1)}, f32[2,256,128]{2,1,0:T(8,128)S(1)}, u32[]{:S(2)}, u32[]{:S(2)}) collective-permute-start(f32[2,256,128]{2,1,0:T(8,128)S(1)} %pad_maximum_fusion.1), channel_id=1, source_target_pairs={{0,1},{1,2},{2,3},{3,4},{4,5},{5,6},{6,7},{7,8},{8,9},{9,10},{10,1... | collective-permute-start | bytes 786440 | tf_op jit(solution)/shard_map/ppermute | solution.py:18
  25.2 0.1 slice_bitcast_fusion.8
  25.3 3.3 %collective-permute-done.1 = f32[2,256,128]{2,1,0:T(8,128)S(1)} collective-permute-done((f32[2,256,128]{2,1,0:T(8,128)S(1)}, f32[2,256,128]{2,1,0:T(8,128)S(1)}, u32[]{:S(2)}, u32[]{:S(2)}) %collective-permute-start.1) | collective-permute-done | bytes 262176 | tf_op jit(solution)/shard_map/ppermute | solution.py:18
  28.6 0.3 fusion.8
  28.8 0.1 broadcast_multiply_fusion
  29.0 1.9 %collective-permute-start.2 = (f32[2,256,128]{2,1,0:T(8,128)S(1)}, f32[2,256,128]{2,1,0:T(8,128)S(1)}, u32[]{:S(2)}, u32[]{:S(2)}) collective-permute-start(f32[2,256,128]{2,1,0:T(8,128)S(1)} %pad_maximum_fusion.2), channel_id=1, source_target_pairs={{1,0},{2,1},{3,2},{4,3},{5,4},{6,5},{7,6},{8,7},{9,8},{10,9},{11,1... | collective-permute-start | bytes 786440 | tf_op jit(solution)/shard_map/ppermute | solution.py:18
  31.0 0.1 slice_bitcast_fusion.5
  31.1 0.1 slice.433
  31.2 0.1 slice.444
  31.4 12.5 %collective-permute-done.2 = f32[2,256,128]{2,1,0:T(8,128)S(1)} collective-permute-done((f32[2,256,128]{2,1,0:T(8,128)S(1)}, f32[2,256,128]{2,1,0:T(8,128)S(1)}, u32[]{:S(2)}, u32[]{:S(2)}) %collective-permute-start.2) | collective-permute-done | bytes 262176 | tf_op jit(solution)/shard_map/ppermute | solution.py:18
  43.9 0.2 fusion.12
  44.0 0.1 maximum_add_fusion.1
  44.2 1.9 %collective-permute-start.3 = (f32[2,256,128]{2,1,0:T(8,128)S(1)}, f32[2,256,128]{2,1,0:T(8,128)S(1)}, u32[]{:S(2)}, u32[]{:S(2)}) collective-permute-start(f32[2,256,128]{2,1,0:T(8,128)S(1)} %pad_maximum_fusion.3), channel_id=1, source_target_pairs={{0,1},{1,2},{2,3},{3,4},{4,5},{5,6},{6,7},{7,8},{8,9},{9,10},{10,1... | collective-permute-start | bytes 786440 | tf_op jit(solution)/shard_map/ppermute | solution.py:18
  46.2 0.1 broadcast_multiply_fusion.1
  46.3 0.1 slice_bitcast_fusion.2
  46.3 3.1 %collective-permute-done.3 = f32[2,256,128]{2,1,0:T(8,128)S(1)} collective-permute-done((f32[2,256,128]{2,1,0:T(8,128)S(1)}, f32[2,256,128]{2,1,0:T(8,128)S(1)}, u32[]{:S(2)}, u32[]{:S(2)}) %collective-permute-start.3) | collective-permute-done | bytes 262176 | tf_op jit(solution)/shard_map/ppermute | solution.py:18
  49.5 0.3 fusion.16
  49.8 0.2 fusion.2
  50.0 0.1 maximum_multiply_fusion
  50.1 6.0 %collective-permute-start.4 = (f32[6,2,32,128]{3,2,1,0:T(8,128)S(1)}, f32[6,2,32,128]{3,2,1,0:T(8,128)S(1)}, u32[]{:S(2)}, u32[]{:S(2)}) collective-permute-start(f32[6,2,32,128]{3,2,1,0:T(8,128)S(1)} %slice.459), channel_id=1, source_target_pairs={{0,32},{32,64},{64,96},{96,128},{128,160},{160,192},{192,224},{224... | collective-permute-start | bytes 589832 | tf_op jit(solution)/shard_map/ppermute | solution.py:24
  56.1 19.4 %collective-permute-done.4 = f32[6,2,32,128]{3,2,1,0:T(8,128)S(1)} collective-permute-done((f32[6,2,32,128]{3,2,1,0:T(8,128)S(1)}, f32[6,2,32,128]{3,2,1,0:T(8,128)S(1)}, u32[]{:S(2)}, u32[]{:S(2)}) %collective-permute-start.4) | collective-permute-done | bytes 196640 | tf_op jit(solution)/shard_map/ppermute | solution.py:24
  75.5 0.1 fusion.21
  75.6 3.6 %collective-permute-start.5 = (f32[6,2,32,128]{3,2,1,0:T(8,128)S(1)}, f32[6,2,32,128]{3,2,1,0:T(8,128)S(1)}, u32[]{:S(2)}, u32[]{:S(2)}) collective-permute-start(f32[6,2,32,128]{3,2,1,0:T(8,128)S(1)} %get-tuple-element.57), channel_id=1, source_target_pairs={{0,480},{32,0},{64,32},{96,64},{128,96},{160,128},{192,160},{224,1... | collective-permute-start | bytes 589832 | tf_op jit(solution)/shard_map/ppermute | solution.py:24
  79.2 4.6 %collective-permute-done.5 = f32[6,2,32,128]{3,2,1,0:T(8,128)S(1)} collective-permute-done((f32[6,2,32,128]{3,2,1,0:T(8,128)S(1)}, f32[6,2,32,128]{3,2,1,0:T(8,128)S(1)}, u32[]{:S(2)}, u32[]{:S(2)}) %collective-permute-start.5) | collective-permute-done | bytes 196640 | tf_op jit(solution)/shard_map/ppermute | solution.py:24
  83.9 0.1 fusion.19
  83.9 0.5 slice.462
  84.4 0.4 reshape.216
  84.8 1.9 %collective-permute-start.6 = (f32[6,2,64,128]{3,2,1,0:T(8,128)S(1)}, f32[6,2,64,128]{3,2,1,0:T(8,128)S(1)}, u32[]{:S(2)}, u32[]{:S(2)}) collective-permute-start(f32[6,2,64,128]{3,2,1,0:T(8,128)S(1)} %reshape.216), channel_id=1, source_target_pairs={{0,128},{32,160},{64,192},{96,224},{128,256},{160,288},{192,320},{... | collective-permute-start | bytes 1179656 | tf_op jit(solution)/shard_map/ppermute | solution.py:24
  86.7 11.7 %collective-permute-done.6 = f32[6,2,64,128]{3,2,1,0:T(8,128)S(1)} collective-permute-done((f32[6,2,64,128]{3,2,1,0:T(8,128)S(1)}, f32[6,2,64,128]{3,2,1,0:T(8,128)S(1)}, u32[]{:S(2)}, u32[]{:S(2)}) %collective-permute-start.6) | collective-permute-done | bytes 393248 | tf_op jit(solution)/shard_map/ppermute | solution.py:24
  98.4 1.5 %reshape.217 = f32[6,2,256,32]{3,2,1,0:T(8,128)} reshape(f32[6,2,64,128]{3,2,1,0:T(8,128)S(1)} %collective-permute-done.6) | data formatting | bytes 786432 | tf_op jit(solution)/shard_map/reshape.115
  99.9 2.8 %fusion.20 = (f32[6,2,256,32]{3,2,1,0:T(8,128)}, f32[6,2,256,32]{3,2,1,0:T(8,128)S(1)}) fusion(f32[6,2,256,128]{3,2,1,0:T(8,128)S(1)} %fusion.19, f32[6,2,256,32]{3,2,1,0:T(8,128)} %reshape.217), kind=kLoop, calls=%fused_computation.84 | loop fusion | flops 98304 | bytes 1572864 | tf_op jit(solution)/shard_map/slice.194
  102.7 1.8 %reshape.218 = f32[6,2,64,128]{3,2,1,0:T(8,128)S(1)} reshape(f32[6,2,256,32]{3,2,1,0:T(8,128)} %get-tuple-element.55) | data formatting | bytes 786432 | tf_op jit(solution)/shard_map/reshape | solution.py:105
  104.5 1.9 %collective-permute-start.7 = (f32[6,2,64,128]{3,2,1,0:T(8,128)S(1)}, f32[6,2,64,128]{3,2,1,0:T(8,128)}, u32[]{:S(2)}, u32[]{:S(2)}) collective-permute-start(f32[6,2,64,128]{3,2,1,0:T(8,128)S(1)} %reshape.218), channel_id=1, source_target_pairs={{0,384},{32,416},{64,448},{96,480},{128,0},{160,32},{192,64},{224,... | collective-permute-start | bytes 1179656 | tf_op jit(solution)/shard_map/ppermute | solution.py:24
  106.5 4.0 %scatter-add.16 = f32[6,2,256,128]{3,2,1,0:T(8,128)S(1)} dynamic-update-slice(f32[6,2,256,128]{3,2,1,0:T(8,128)S(1)} %fusion.19, f32[6,2,256,32]{3,2,1,0:T(8,128)S(1)} %get-tuple-element.56, s32[]{:T(128)} %constant.132.clone.1, s32[]{:T(128)} %constant.132.clone.1, s32[]{:T(128)} %constant.132.clone.1, s32[]{:T(128)} %constant.132.clone.1) | dynamic-update-slice | bytes 786436 | tf_op jit(solution)/shard_map/scatter-add | solution.py:108
  110.5 0.0 copy-start
  110.5 5.6 %collective-permute-done.7 = f32[6,2,64,128]{3,2,1,0:T(8,128)} collective-permute-done((f32[6,2,64,128]{3,2,1,0:T(8,128)S(1)}, f32[6,2,64,128]{3,2,1,0:T(8,128)}, u32[]{:S(2)}, u32[]{:S(2)}) %collective-permute-start.7) | collective-permute-done | bytes 393248 | tf_op jit(solution)/shard_map/ppermute | solution.py:24
  116.1 2.5 %reshape.219 = f32[6,2,256,32]{3,2,1,0:T(8,128)} reshape(f32[6,2,64,128]{3,2,1,0:T(8,128)} %collective-permute-done.7) | data formatting | bytes 786432 | tf_op jit(solution)/shard_map/reshape.127
  118.6 1.9 %fusion = f32[1,6,2,256,32]{4,3,2,1,0:T(8,128)S(1)} fusion(f32[6,2,256,32]{3,2,1,0:T(8,128)} %reshape.219, f32[6,2,256,128]{3,2,1,0:T(8,128)S(1)} %scatter-add.16), kind=kLoop, calls=%fused_computation.1 | loop fusion | flops 98304 | bytes 1179648 | tf_op jit(solution)/shard_map/broadcast_in_dim | solution.py:110
  120.5 0.0 copy-done
  120.5 8.8 %scatter-add.19 = f32[1,6,2,256,128]{4,3,2,1,0:T(8,128)} dynamic-update-slice(f32[1,6,2,256,128]{4,3,2,1,0:T(8,128)} %bitcast.161, f32[1,6,2,256,32]{4,3,2,1,0:T(8,128)S(1)} %fusion, s32[]{:T(128)} %constant.132.clone.1, s32[]{:T(128)} %constant.132.clone.1, s32[]{:T(128)} %constant.132.clone.1, s32[]{:T(128)} %constant.132.clone.1, s32[]{:T(128)} %constant.134.clone.1) | dynamic-update-slice | bytes 786436 | tf_op jit(solution)/shard_map/scatter-add | solution.py:109
  (19 shorter events, 0.4 us)
Async XLA Ops:
  2.5 19.1 %collective-permute-start = (f32[2,256,128]{2,1,0:T(8,128)S(1)}, f32[2,256,128]{2,1,0:T(8,128)S(1)}, u32[]{:S(2)}, u32[]{:S(2)}) collective-permute-start(f32[2,256,128]{2,1,0:T(8,128)S(1)} %pad_maximum_fusion), channel_id=1, source_target_pairs={{1,0},{2,1},{3,2},{4,3},{5,4},{6,5},{7,6},{8,7},{9,8},{10,9},{11,1... | collective-permute-start | bytes 786440 | tf_op jit(solution)/shard_map/ppermute | solution.py:18
  21.7 1.4 %copy-start.1 = (f32[1,6,2,256,128]{4,3,2,1,0:T(8,128)S(1)}, f32[1,6,2,256,128]{4,3,2,1,0:T(8,128)}, u32[]{:S(2)}) copy-start(f32[1,6,2,256,128]{4,3,2,1,0:T(8,128)} %param.12) | copy-start | bytes 4718596
  23.3 5.3 %collective-permute-start.1 = (f32[2,256,128]{2,1,0:T(8,128)S(1)}, f32[2,256,128]{2,1,0:T(8,128)S(1)}, u32[]{:S(2)}, u32[]{:S(2)}) collective-permute-start(f32[2,256,128]{2,1,0:T(8,128)S(1)} %pad_maximum_fusion.1), channel_id=1, source_target_pairs={{0,1},{1,2},{2,3},{3,4},{4,5},{5,6},{6,7},{7,8},{8,9},{9,10},{10,1... | collective-permute-start | bytes 786440 | tf_op jit(solution)/shard_map/ppermute | solution.py:18
  29.0 14.8 %collective-permute-start.2 = (f32[2,256,128]{2,1,0:T(8,128)S(1)}, f32[2,256,128]{2,1,0:T(8,128)S(1)}, u32[]{:S(2)}, u32[]{:S(2)}) collective-permute-start(f32[2,256,128]{2,1,0:T(8,128)S(1)} %pad_maximum_fusion.2), channel_id=1, source_target_pairs={{1,0},{2,1},{3,2},{4,3},{5,4},{6,5},{7,6},{8,7},{9,8},{10,9},{11,1... | collective-permute-start | bytes 786440 | tf_op jit(solution)/shard_map/ppermute | solution.py:18
  44.2 5.2 %collective-permute-start.3 = (f32[2,256,128]{2,1,0:T(8,128)S(1)}, f32[2,256,128]{2,1,0:T(8,128)S(1)}, u32[]{:S(2)}, u32[]{:S(2)}) collective-permute-start(f32[2,256,128]{2,1,0:T(8,128)S(1)} %pad_maximum_fusion.3), channel_id=1, source_target_pairs={{0,1},{1,2},{2,3},{3,4},{4,5},{5,6},{6,7},{7,8},{8,9},{9,10},{10,1... | collective-permute-start | bytes 786440 | tf_op jit(solution)/shard_map/ppermute | solution.py:18
  50.1 25.4 %collective-permute-start.4 = (f32[6,2,32,128]{3,2,1,0:T(8,128)S(1)}, f32[6,2,32,128]{3,2,1,0:T(8,128)S(1)}, u32[]{:S(2)}, u32[]{:S(2)}) collective-permute-start(f32[6,2,32,128]{3,2,1,0:T(8,128)S(1)} %slice.459), channel_id=1, source_target_pairs={{0,32},{32,64},{64,96},{96,128},{128,160},{160,192},{192,224},{224... | collective-permute-start | bytes 589832 | tf_op jit(solution)/shard_map/ppermute | solution.py:24
  75.6 8.3 %collective-permute-start.5 = (f32[6,2,32,128]{3,2,1,0:T(8,128)S(1)}, f32[6,2,32,128]{3,2,1,0:T(8,128)S(1)}, u32[]{:S(2)}, u32[]{:S(2)}) collective-permute-start(f32[6,2,32,128]{3,2,1,0:T(8,128)S(1)} %get-tuple-element.57), channel_id=1, source_target_pairs={{0,480},{32,0},{64,32},{96,64},{128,96},{160,128},{192,160},{224,1... | collective-permute-start | bytes 589832 | tf_op jit(solution)/shard_map/ppermute | solution.py:24
  84.8 13.6 %collective-permute-start.6 = (f32[6,2,64,128]{3,2,1,0:T(8,128)S(1)}, f32[6,2,64,128]{3,2,1,0:T(8,128)S(1)}, u32[]{:S(2)}, u32[]{:S(2)}) collective-permute-start(f32[6,2,64,128]{3,2,1,0:T(8,128)S(1)} %reshape.216), channel_id=1, source_target_pairs={{0,128},{32,160},{64,192},{96,224},{128,256},{160,288},{192,320},{... | collective-permute-start | bytes 1179656 | tf_op jit(solution)/shard_map/ppermute | solution.py:24
  104.5 11.6 %collective-permute-start.7 = (f32[6,2,64,128]{3,2,1,0:T(8,128)S(1)}, f32[6,2,64,128]{3,2,1,0:T(8,128)}, u32[]{:S(2)}, u32[]{:S(2)}) collective-permute-start(f32[6,2,64,128]{3,2,1,0:T(8,128)S(1)} %reshape.218), channel_id=1, source_target_pairs={{0,384},{32,416},{64,448},{96,480},{128,0},{160,32},{192,64},{224,... | collective-permute-start | bytes 1179656 | tf_op jit(solution)/shard_map/ppermute | solution.py:24
  110.5 10.0 %copy-start = (f32[6,2,256,128]{3,2,1,0:T(8,128)}, f32[6,2,256,128]{3,2,1,0:T(8,128)S(1)}, u32[]{:S(2)}) copy-start(f32[6,2,256,128]{3,2,1,0:T(8,128)S(1)} %scatter-add.16) | copy-start | bytes 4718596
where the time goes:
time: 131 us; the launch traced here: 129 us
  waiting for transfers between devices  76.4 us (58%)
  local copies, waits for them, and re-layouts  21.9 us (17%)
  starting transfers between devices  21.8 us (17%)
  other arithmetic  8.95 us (7%)
    ppermute x4, waiting for transfers between devices, from_behind(): return lax.ppermute(value, axis, pairs)  41.3 us
    ppermute x4, waiting for transfers between devices, passed_along(): return lax.ppermute(block, axis, route)  35 us
    ppermute x4, starting transfers between devices, from_behind(): return lax.ppermute(value, axis, pairs)  13.5 us
    scatter-add x1, local copies, waits for them, and re-layouts, on_device(): result = result.at[..., size_y - BAND:].add(from_above)  8.83 us
    ppermute x4, starting transfers between devices, passed_along(): return lax.ppermute(block, axis, route)  8.35 us
    another operation x2, local copies, waits for them, and re-layouts  4.04 us
    scatter-add x1, local copies, waits for them, and re-layouts, on_device(): result = combined.at[..., :BAND].add(from_below)  4.03 us
    another operation x2, other arithmetic  2.88 us
  transfers between devices with their start and end apart: 8, of which 8 were waited for; matrix products, arithmetic and copies ran while one was open for 4% of the time, Pallas kernels for 0%

commit v1 on v0

v1 whole, which is shorter than its diff:
```python
import functools
import math

import jax
import jax.numpy as jnp
from jax import lax
from jax.experimental import pallas as pl
from jax.experimental.pallas import tpu as pltpu
from jax.sharding import PartitionSpec as P

BAND = 32
MESH = pl.DeviceIdType.MESH
MAGNETIC = 0.5
TX = 256
TY = 128
PAD = 8
ROWS = 32
EX, EY, EZ, HX, HY, HZ = range(6)

EARLY = ((HX, 0), (HY, 0), (HZ, 0), (HZ, 1), (EZ, 0))
LATE = ((HX, 1), (HY, 1), (EX, 0), (EY, 0), (EX, 1), (EY, 1), (EZ, 1))
ORDER = EARLY + LATE
GROUPS = ((0, len(EARLY)), (len(EARLY), len(LATE)))


def row_tiles(body):
    def step(index, carry):
        body(pl.multiple_of(index * ROWS, ROWS))
        return carry

    lax.fori_loop(0, TX // ROWS, step, 0)


def planes_of(group, body):
    first, count = GROUPS[group]

    def step(index, carry):
        body(index)
        return carry

    lax.fori_loop(first, first + count, step, 0)


def kernel(
    tiles, subs, decay, coupling, seeds, material, out,
    field, mat, ca, cb, s0, s1, h1, h2, e1, a1, a2, up_in, down_in, w,
    yc_out, yn_out, xn_out, xc_out, yc_in, yn_in, xn_in, xc_in,
    load_sem, store_sem, depth_send, depth_recv, band_send, band_recv,
):
    tile = lax.axis_index("tile")
    sub = lax.axis_index("sub")
    side = math.isqrt(tiles)
    has_below = sub > 0
    has_above = sub < subs - 1
    below = jnp.maximum(sub - 1, 0)
    above = jnp.minimum(sub + 1, subs - 1)
    x_prev = lax.rem(tile + tiles - 1, tiles)
    x_next = lax.rem(tile + 1, tiles)
    y_prev = lax.rem(tile + tiles - side, tiles)
    y_next = lax.rem(tile + side, tiles)

    loads = [
        pltpu.make_async_copy(material.at[0], mat, load_sem.at[0]),
        pltpu.make_async_copy(seeds.at[0, 0:3], field.at[0:3, :, PAD : PAD + TX], load_sem.at[1]),
        pltpu.make_async_copy(seeds.at[0, 3:6], field.at[3:6, :, PAD : PAD + TX], load_sem.at[2]),
    ]
    for load in loads:
        load.start()

    barrier = pltpu.get_barrier_semaphore()

    def greet(other_tile, other_sub):
        pl.semaphore_signal(barrier, inc=1, device_id=(other_tile, other_sub), device_id_type=MESH)

    for other in (x_prev, x_next, y_prev, y_next):
        greet(other, sub)
    pl.when(has_below)(lambda: greet(tile, below))
    pl.when(has_above)(lambda: greet(tile, above))

    lane = lax.broadcasted_iota(jnp.int32, (ROWS, TY), 1)
    not_last = lane < TY - 1
    not_first = lane > 0
    zeros_pad = jnp.zeros((PAD, TY), jnp.float32)
    for comp in range(3):
        for plane in range(2):
            for buf in (s0, s1):
                buf[comp, plane, PAD + TX : PAD + TX + PAD, :] = zeros_pad
            for buf in (h1, h2):
                buf[comp, plane, 0:PAD, :] = zeros_pad

    def at(buf, comp, plane, row):
        return buf[comp, plane, pl.ds(PAD + row, ROWS), :]

    def put(buf, comp, plane, row, value):
        buf[comp, plane, pl.ds(PAD + row, ROWS), :] = value

    def plus_x(buf, comp, plane, row):
        return buf[comp, plane, pl.ds(PAD + row + 1, ROWS), :] - at(buf, comp, plane, row)

    def minus_x(buf, comp, plane, row):
        return at(buf, comp, plane, row) - buf[comp, plane, pl.ds(PAD + row - 1, ROWS), :]

    def plus_y(value):
        return jnp.where(not_last, pltpu.roll(value, TY - 1, 1), 0.0) - value

    def minus_y(value):
        return value - jnp.where(not_first, pltpu.roll(value, 1, 1), 0.0)

    def curl_z(buf, plane, row):
        return plus_x(buf, 1, plane, row) - plus_y(at(buf, 0, plane, row))

    ramp_lane = lane.astype(jnp.float32) + 0.5
    ramp_y = jnp.minimum(jnp.minimum(ramp_lane, TY - ramp_lane) * (1.0 / BAND), 1.0)
    row_iota = lax.broadcasted_iota(jnp.int32, (ROWS, TY), 0)

    def weight(row):
        position = (row_iota + row).astype(jnp.float32) + 0.5
        return jnp.minimum(jnp.minimum(position, TX - position) * (1.0 / BAND), 1.0) * ramp_y

    def rows_of(buf, index, row):
        return buf[index, pl.ds(row, ROWS), :]

    def depth_copy(turn, upward):
        source = (a1, a2)[turn] if upward else (s0, s1)[turn].at[0:2, 0, PAD : PAD + TX]
        target = (up_in if upward else down_in).at[turn]
        slot = turn * 2 + int(upward)
        return pltpu.make_async_remote_copy(
            source, target, depth_send.at[slot], depth_recv.at[slot],
            device_id=(tile, above if upward else below), device_id_type=MESH)

    def band_copy(kind, group, toward_next):
        first, count = GROUPS[group]
        source, target = ((yc_out, yc_in), (xn_out, xn_in), (yn_out, yn_in), (xc_out, xc_in))[kind]
        direction = int(toward_next)
        if kind in (0, 2):
            other = y_next if toward_next else y_prev
        else:
            other = x_next if toward_next else x_prev
        slot = (kind * 2 + group) * 2 + direction
        part = slice(first, first + count)
        return pltpu.make_async_remote_copy(
            source.at[direction, part], target.at[direction, part],
            band_send.at[slot], band_recv.at[slot],
            device_id=(other, sub), device_id_type=MESH)

    def send_band(kind, group):
        for toward_next in (False, True):
            band_copy(kind, group, toward_next).start()

    def wait_band(kind, group):
        for toward_next in (False, True):
            band_copy(kind, group, toward_next).wait_recv()

    loads[0].wait()
    loads[1].wait()
    d0, d1, d2, d3 = (decay[i] for i in range(4))
    c0, c1, c2, c3 = (coupling[i] for i in range(4))

    def scale(row):
        for plane in range(2):
            label = mat[plane, pl.ds(row, ROWS), :]
            is0, is1, is2 = label == 0, label == 1, label == 2
            couple = jnp.where(is0, c0, jnp.where(is1, c1, jnp.where(is2, c2, c3)))
            cb[plane, pl.ds(row, ROWS), :] = couple
            ca[plane, pl.ds(row, ROWS), :] = jnp.where(is0, d0, jnp.where(is1, d1, jnp.where(is2, d2, d3)))
            for comp in range(3):
                put(s0, comp, plane, row, couple * at(field, comp, plane, row))

    row_tiles(scale)
    pl.semaphore_wait(barrier, 4 + has_below.astype(jnp.int32) + has_above.astype(jnp.int32))
    pl.when(has_below)(lambda: depth_copy(0, False).start())
    loads[2].wait()

    def partial(hbuf, offset, sbuf, abuf):
        def body(row):
            s_x, s_y, s_z = (at(sbuf, comp, 1, row) for comp in range(3))
            abuf[0, pl.ds(row, ROWS), :] = at(hbuf, offset, 1, row) + plus_y(s_z) + s_y
            abuf[1, pl.ds(row, ROWS), :] = at(hbuf, offset + 1, 1, row) - s_x - plus_x(sbuf, 2, 1, row)

        row_tiles(body)

    partial(field, HX, s0, a1)
    pl.when(has_above)(lambda: depth_copy(0, True).start())

    def magnetic_local(hbuf, offset, sbuf, row):
        s_x0, s_y0, s_z0 = (at(sbuf, comp, 0, row) for comp in range(3))
        new_x = at(hbuf, offset, 0, row) + plus_y(s_z0) - (at(sbuf, 1, 1, row) - s_y0)
        new_y = at(hbuf, offset + 1, 0, row) + (at(sbuf, 0, 1, row) - s_x0) - plus_x(sbuf, 2, 0, row)
        new_z = at(hbuf, offset + 2, 0, row) + curl_z(sbuf, 0, row)
        new_z1 = at(hbuf, offset + 2, 1, row) + curl_z(sbuf, 1, row)
        return new_x, new_y, new_z, new_z1

    def first_local(row):
        new_x, new_y, new_z, new_z1 = magnetic_local(field, HX, s0, row)
        put(h1, 0, 0, row, new_x)
        put(h1, 1, 0, row, new_y)
        put(h1, 2, 0, row, new_z)
        put(h1, 2, 1, row, new_z1)

    row_tiles(first_local)

    def edge_planes(turn, sbuf):
        @pl.when(jnp.logical_not(has_above))
        def _():
            def body(row):
                for comp in range(2):
                    down_in[turn, comp, pl.ds(row, ROWS), :] = jnp.zeros((ROWS, TY), jnp.float32)

            row_tiles(body)

        @pl.when(jnp.logical_not(has_below))
        def _():
            def body(row):
                up_in[turn, 0, pl.ds(row, ROWS), :] = at(sbuf, 1, 0, row)
                up_in[turn, 1, pl.ds(row, ROWS), :] = -at(sbuf, 0, 0, row)

            row_tiles(body)

    def wait_depth(turn):
        pl.when(has_above)(lambda: depth_copy(turn, False).wait_recv())
        pl.when(has_below)(lambda: depth_copy(turn, True).wait_recv())

    def magnetic_rest(turn, abuf, sbuf, row):
        new_x = rows_of(abuf, 0, row) - down_in[turn, 1, pl.ds(row, ROWS), :]
        new_y = rows_of(abuf, 1, row) + down_in[turn, 0, pl.ds(row, ROWS), :]
        under_x = up_in[turn, 0, pl.ds(row, ROWS), :] - at(sbuf, 1, 0, row)
        under_y = up_in[turn, 1, pl.ds(row, ROWS), :] + at(sbuf, 0, 0, row)
        return new_x, new_y, under_x, under_y

    def electric_xy(ebuf, hbuf, plane, row, h_x, h_y, under_x, under_y):
        h_z = at(hbuf, 2, plane, row)
        decays = rows_of(ca, plane, row)
        new_x = decays * at(ebuf, 0, plane, row) - MAGNETIC * (minus_y(h_z) - (h_y - under_y))
        new_y = decays * at(ebuf, 1, plane, row) - MAGNETIC * ((h_x - under_x) - minus_x(hbuf, 2, plane, row))
        return new_x, new_y

    def electric_z(ebuf, hbuf, plane, row, h_x):
        decays = rows_of(ca, plane, row)
        return decays * at(ebuf, 2, plane, row) - MAGNETIC * (minus_x(hbuf, 1, plane, row) - minus_y(h_x))

    edge_planes(0, s0)
    wait_depth(0)

    def first_rest(row):
        x1, y1, under_x, under_y = magnetic_rest(0, a1, s0, row)
        put(h1, 0, 1, row, x1)
        put(h1, 1, 1, row, y1)
        x0, y0 = at(h1, 0, 0, row), at(h1, 1, 0, row)
        for plane, (h_x, h_y, b_x, b_y) in enumerate(((x0, y0, under_x, under_y), (x1, y1, x0, y0))):
            new = (*electric_xy(field, h1, plane, row, h_x, h_y, b_x, b_y), electric_z(field, h1, plane, row, h_x))
            couple = rows_of(cb, plane, row)
            for comp in range(3):
                put(e1, comp, plane, row, new[comp])
                put(s1, comp, plane, row, couple * new[comp])

    row_tiles(first_rest)
    pl.when(has_below)(lambda: depth_copy(1, False).start())
    partial(h1, 0, s1, a2)
    pl.when(has_above)(lambda: depth_copy(1, True).start())

    def keep(name, row, value, weights):
        w[ORDER.index(name), pl.ds(row, ROWS), :] = value * weights

    def second_local(row):
        new_x, new_y, new_z, new_z1 = magnetic_local(h1, 0, s1, row)
        put(h2, 0, 0, row, new_x)
        put(h2, 1, 0, row, new_y)
        put(h2, 2, 0, row, new_z)
        put(h2, 2, 1, row, new_z1)
        weights = weight(row)
        keep((HX, 0), row, new_x, weights)
        keep((HY, 0), row, new_y, weights)
        keep((HZ, 0), row, new_z, weights)
        keep((HZ, 1), row, new_z1, weights)
        keep((EZ, 0), row, electric_z(e1, h2, 0, row, new_x), weights)

    row_tiles(second_local)

    def slot_of(rows):
        return lax.broadcasted_iota(jnp.int32, (rows, TY), 1) // BAND

    def pack_lanes(values):
        slot = slot_of(values[0].shape[0])
        turned = [values[0]] + [pltpu.roll(values[k], BAND * k, 1) for k in (1, 2, 3)]
        low, high = turned[3], turned[0]
        for k in (2, 1, 0):
            low = jnp.where(slot == k, turned[k], low)
            high = jnp.where(slot == k, turned[k + 1], high)
        return low, high

    def unpack_lanes(low_side, high_side):
        slot = slot_of(low_side.shape[0])
        turned = []
        for k in range(4):
            mixed = jnp.where(slot == (k + 3) % 4, low_side, high_side)
            shift = (TY - BAND * (k - 1)) % TY
            turned.append(pltpu.roll(mixed, shift, 1) if shift else mixed)
        return [jnp.where(slot == 0, turned[k], jnp.where(slot == 3, turned[(k + 2) % 4], 0.0)) for k in range(4)]

    corner_rows = (0, 16, TX - 32, TX - 16)
    middle_rows = (32, 80, 128, 176)

    def middle_lanes():
        slot = slot_of(16)
        return jnp.logical_or(slot == 1, slot == 2)

    def pack_corners(index):
        values = [w[index, first : first + 16, :] for first in corner_rows]
        low, high = pack_lanes(values)
        yc_out[0, index], yc_out[1, index] = low, high
        middle = middle_lanes()
        for direction in range(2):
            xn_out[direction, index] = jnp.where(
                middle, values[2 * direction], pltpu.roll(values[2 * direction + 1], TY // 2, 1))

    def pack_middle(index):
        low, high = pack_lanes([w[index, first : first + 48, :] for first in middle_rows])
        yn_out[0, index], yn_out[1, index] = low, high

    def add_corners(index):
        added = unpack_lanes(yc_in[1, index], yc_in[0, index])
        values = []
        for first, more in zip(corner_rows, added):
            total = w[index, first : first + 16, :] + more
            w[index, first : first + 16, :] = total
            values.append(total)
        middle = middle_lanes()
        for direction in range(2):
            xc_out[direction, index] = jnp.where(
                middle, pltpu.roll(values[2 * direction + 1], TY // 2, 1), values[2 * direction])

    def add_middle(index):
        added = unpack_lanes(yn_in[1, index], yn_in[0, index])
        for first, more in zip(middle_rows, added):
            w[index, first : first + 48, :] += more

    def add_x_bands(index):
        middle = middle_lanes()
        for side_of, first in ((1, 0), (0, TX - 32)):
            plain, summed = xn_in[side_of, index], xc_in[side_of, index]
            w[index, first : first + 16, :] += jnp.where(middle, plain, summed)
            w[index, first + 16 : first + 32, :] += pltpu.roll(jnp.where(middle, summed, plain), TY // 2, 1)

    def send_group(group):
        planes_of(group, pack_corners)
        send_band(0, group)
        send_band(1, group)
        planes_of(group, pack_middle)
        send_band(2, group)

    send_group(0)
    edge_planes(1, s1)
    wait_depth(1)

    def second_rest(row):
        x1, y1, under_x, under_y = magnetic_rest(1, a2, s1, row)
        put(h2, 0, 1, row, x1)
        put(h2, 1, 1, row, y1)
        x0, y0 = at(h2, 0, 0, row), at(h2, 1, 0, row)
        weights = weight(row)
        keep((HX, 1), row, x1, weights)
        keep((HY, 1), row, y1, weights)
        for plane, (h_x, h_y, b_x, b_y) in enumerate(((x0, y0, under_x, under_y), (x1, y1, x0, y0))):
            new_x, new_y = electric_xy(e1, h2, plane, row, h_x, h_y, b_x, b_y)
            keep((EX, plane), row, new_x, weights)
            keep((EY, plane), row, new_y, weights)
        keep((EZ, 1), row, electric_z(e1, h2, 1, row, x1), weights)

    row_tiles(second_rest)
    send_group(1)

    for group in range(2):
        wait_band(0, group)
        planes_of(group, add_corners)
        send_band(3, group)

    stores = []
    for group in range(2):
        wait_band(2, group)
        planes_of(group, add_middle)
        wait_band(1, group)
        wait_band(3, group)
        planes_of(group, add_x_bands)
        first, count = GROUPS[group]
        for index in range(first, first + count):
            comp, plane = ORDER[index]
            store = pltpu.make_async_copy(w.at[index], out.at[0, comp, plane], store_sem.at[index])
            store.start()
            stores.append(store)

    for turn in range(2):
        pl.when(has_below)(lambda: depth_copy(turn, False).wait_send())
        pl.when(has_above)(lambda: depth_copy(turn, True).wait_send())
    for group in range(2):
        for kind in range(4):
            for toward_next in (False, True):
                band_copy(kind, group, toward_next).wait_send()
    for store in stores:
        store.wait()


def on_device(tiles, subs, seeds, material, decay, coupling):
    f32 = jnp.float32
    padded = (3, 2, PAD + TX + PAD, TY)
    planes = len(ORDER)
    narrow, wide = pltpu.VMEM((2, planes, 16, TY), f32), pltpu.VMEM((2, planes, 48, TY), f32)
    smem = pl.BlockSpec(memory_space=pltpu.SMEM)
    anywhere = pl.BlockSpec(memory_space=pl.ANY)
    return pl.pallas_call(
        functools.partial(kernel, tiles, subs),
        out_shape=jax.ShapeDtypeStruct(seeds.shape, f32),
        in_specs=[smem, smem, anywhere, anywhere],
        out_specs=anywhere,
        scratch_shapes=[
            pltpu.VMEM((6, *padded[1:]), f32),
            pltpu.VMEM((2, TX, TY), jnp.int32),
            pltpu.VMEM((2, TX, TY), f32),
            pltpu.VMEM((2, TX, TY), f32),
            *[pltpu.VMEM(padded, f32)] * 5,
            pltpu.VMEM((2, TX, TY), f32),
            pltpu.VMEM((2, TX, TY), f32),
            pltpu.VMEM((2, 2, TX, TY), f32),
            pltpu.VMEM((2, 2, TX, TY), f32),
            pltpu.VMEM((planes, TX, TY), f32),
            narrow, wide, narrow, narrow,
            narrow, wide, narrow, narrow,
            pltpu.SemaphoreType.DMA((3,)),
            pltpu.SemaphoreType.DMA((planes,)),
            pltpu.SemaphoreType.DMA((4,)),
            pltpu.SemaphoreType.DMA((4,)),
            pltpu.SemaphoreType.DMA((16,)),
            pltpu.SemaphoreType.DMA((16,)),
        ],
        compiler_params=pltpu.CompilerParams(collective_id=0, has_side_effects=True),
    )(decay, coupling, seeds, material)


def solution(mesh):
    placed = (P("tile", None, "sub", None, None), P("tile", "sub", None, None), P(), P())
    return jax.shard_map(
        functools.partial(on_device, mesh.shape["tile"], mesh.shape["sub"]),
        mesh=mesh,
        in_specs=placed,
        out_specs=P("tile", None, "sub", None, None),
        check_vma=False,
    )
```

time: 131 us -> 64.8 us (0.49); the launches traced: 129 us -> 64.6 us
  waiting for transfers between devices: 76.4 us -> 0 us
  Pallas kernels: 0 us -> 61.9 us
  starting transfers between devices: 21.8 us -> 0 us
  local copies, waits for them, and re-layouts: 21.9 us -> 2.65 us
  other arithmetic: 8.95 us -> 0 us
    ppermute x8 -> x0, waiting for transfers between devices: 76.4 us -> none  [the longest x4 41.3 us: from_behind(): return lax.ppermute(value, axis, pairs)]
    pallas_call x0 -> x1, Pallas kernels: none -> 61.9 us  [on_device(): pl.pallas_call(functools.partial(kernel, tiles, subs), out_shape=jax.Shap...]
    ppermute x8 -> x0, starting transfers between devices: 21.8 us -> none  [the longest x4 13.5 us: from_behind(): return lax.ppermute(value, axis, pairs)]
    scatter-add x2 -> x0, local copies, waits for them, and re-layouts: 12.9 us -> none  [the longest x1 8.83 us: on_device(): result = result.at[..., size_y - BAND:].add(from_above)]
    another operation x2 -> x0, local copies, waits for them, and re-layouts: 4.04 us -> none
    another operation x10 -> x0, other arithmetic: 3.83 us -> none
    reshape x2 -> x0, local copies, waits for them, and re-layouts: 2.17 us -> none  [the longest x1 1.79 us: on_device(): bottom_slab = combined[..., :BAND].reshape(6, depth, flat_rows, 128)]
    broadcast_in_dim x1 -> x0, other arithmetic: 1.88 us -> none  [on_device(): return result[None]]
  transfers between devices with their start and end apart: 8 -> 0, of which waited for: 8 -> 0; matrix products, arithmetic and copies ran while one was open for 4% -> 0% of each run, Pallas kernels for 0% -> 0%
where the time goes in v1:
time: 64.8 us; the launch traced here: 64.6 us
  Pallas kernels  61.9 us (96%)
  local copies, waits for them, and re-layouts  2.65 us (4%)
    pallas_call x1, Pallas kernels, on_device(): pl.pallas_call(functools.partial(kernel, tiles, subs), out_shape=jax.Shap...  61.9 us
    unnamed x1, local copies, waits for them, and re-layouts  2.65 us

profile of v1, /device:TPU:7, one launch (start us, length us, event | category | flops | bytes accessed | tf_op | source)
XLA Modules:
  0.0 64.6 jit_solution(2351022363639493287)
XLA Ops:
  0.0 61.9 %shard_map.46 = f32[1,6,2,256,128]{4,3,2,1,0:T(8,128)} custom-call(f32[4]{0:T(128)} %decay.1, f32[4]{0:T(128)} %coupling.1, f32[1,6,2,256,128]{4,3,2,1,0:T(8,128)} %seeds.1, s32[1,2,256,128]{3,2,1,0:T(8,128)} %material.1), custom_call_target="tpu_custom_call" | custom-call | tf_op jit(solution)/shard_map/pallas_call | solution.py:409
  61.9 2.7 %copy.6 = f32[1,6,2,256,128]{4,3,2,1,0:T(8,128)} copy(f32[1,6,2,256,128]{4,3,2,1,0:T(8,128)} %shard_map.46) | data formatting | bytes 3145728

commit v2 on v1

--- a/solution.py
+++ b/solution.py
@@ -22,6 +22,11 @@
 ORDER = EARLY + LATE
 GROUPS = ((0, len(EARLY)), (len(EARLY), len(LATE)))
 
+RUN = 8
+PARTS = 3
+PART_ROWS = 56
+DIRECT = TX - PARTS * PART_ROWS
+
 
 def row_tiles(body):
     def step(index, carry):
@@ -42,10 +47,10 @@
 
 
 def kernel(
-    tiles, subs, decay, coupling, seeds, material, out,
-    field, mat, ca, cb, s0, s1, h1, h2, e1, a1, a2, up_in, down_in, w,
+    tiles, subs, decay_in, coupling_in, seeds, material, w,
+    decay, coupling, field, mat, ca, cb, s0, s1, h1, h2, e1, a1, a2, up_in, down_in, relay_in,
     yc_out, yn_out, xn_out, xc_out, yc_in, yn_in, xn_in, xc_in,
-    load_sem, store_sem, depth_send, depth_recv, band_send, band_recv,
+    load_sem, depth_send, depth_recv, part_send, part_recv, relay_recv, relay_send, band_send, band_recv,
 ):
     tile = lax.axis_index("tile")
     sub = lax.axis_index("sub")
@@ -63,6 +68,8 @@
         pltpu.make_async_copy(material.at[0], mat, load_sem.at[0]),
         pltpu.make_async_copy(seeds.at[0, 0:3], field.at[0:3, :, PAD : PAD + TX], load_sem.at[1]),
         pltpu.make_async_copy(seeds.at[0, 3:6], field.at[3:6, :, PAD : PAD + TX], load_sem.at[2]),
+        pltpu.make_async_copy(decay_in, decay, load_sem.at[3]),
+        pltpu.make_async_copy(coupling_in, coupling, load_sem.at[4]),
     ]
     for load in loads:
         load.start()
@@ -76,6 +83,47 @@
         greet(other, sub)
     pl.when(has_below)(lambda: greet(tile, below))
     pl.when(has_above)(lambda: greet(tile, above))
+    place_in_run = lax.rem(sub, RUN)
+    start = sub - place_in_run
+    run_above = start + RUN < subs
+    run_below = start > 0
+    crosses_up = jnp.logical_and(place_in_run == RUN - 1, run_above)
+    crosses_down = jnp.logical_and(place_in_run == 0, run_below)
+    odd = lax.rem(place_in_run, 2) == 1
+    relays_up = jnp.logical_and(jnp.logical_and(odd, place_in_run < RUN - 1), run_above)
+    relays_down = jnp.logical_and(jnp.logical_and(jnp.logical_not(odd), place_in_run > 0), run_below)
+    relay_part = jnp.where(odd, place_in_run // 2, jnp.maximum(place_in_run // 2 - 1, 0))
+    last_here = start + RUN - 1
+    first_above = jnp.minimum(start + RUN, subs - 1)
+    last_below = jnp.maximum(start - 1, 0)
+
+    def up_relay(part):
+        return start + 2 * part + 1
+
+    def down_relay(part):
+        return start + 2 * part + 2
+
+    @pl.when(crosses_up)
+    def _():
+        for part in range(PARTS):
+            greet(tile, up_relay(part))
+            greet(tile, jnp.minimum(down_relay(part) + RUN, subs - 1))
+
+    @pl.when(crosses_down)
+    def _():
+        for part in range(PARTS):
+            greet(tile, down_relay(part))
+            greet(tile, jnp.maximum(up_relay(part) - RUN, 0))
+
+    @pl.when(relays_up)
+    def _():
+        greet(tile, last_here)
+        greet(tile, first_above)
+
+    @pl.when(relays_down)
+    def _():
+        greet(tile, start)
+        greet(tile, last_below)
 
     lane = lax.broadcasted_iota(jnp.int32, (ROWS, TY), 1)
     not_last = lane < TY - 1
@@ -120,13 +168,75 @@
     def rows_of(buf, index, row):
         return buf[index, pl.ds(row, ROWS), :]
 
-    def depth_copy(turn, upward):
-        source = (a1, a2)[turn] if upward else (s0, s1)[turn].at[0:2, 0, PAD : PAD + TX]
-        target = (up_in if upward else down_in).at[turn]
+    def depth_rows(turn, upward, first, count):
+        if upward:
+            return (a1, a2)[turn].at[:, first : first + count]
+        return (s0, s1)[turn].at[0:2, 0, PAD + first : PAD + first + count]
+
+    def depth_copy(turn, upward, count):
         slot = turn * 2 + int(upward)
         return pltpu.make_async_remote_copy(
-            source, target, depth_send.at[slot], depth_recv.at[slot],
+            depth_rows(turn, upward, 0, count), (up_in if upward else down_in).at[turn, :, 0:count],
+            depth_send.at[slot], depth_recv.at[slot],
             device_id=(tile, above if upward else below), device_id_type=MESH)
+
+    def part_copy(turn, upward, part):
+        relay = up_relay(part) if upward else down_relay(part)
+        return pltpu.make_async_remote_copy(
+            depth_rows(turn, upward, DIRECT + part * PART_ROWS, PART_ROWS), relay_in.at[turn],
+            part_send.at[turn * PARTS + part], relay_recv.at[turn],
+            device_id=(tile, relay), device_id_type=MESH)
+
+    def relay_copy(turn, upward, part):
+        target = (up_in if upward else down_in).at[
+            turn, :, pl.ds(pl.multiple_of(DIRECT + part * PART_ROWS, 8), PART_ROWS)]
+        return pltpu.make_async_remote_copy(
+            relay_in.at[turn], target, relay_send.at[turn], part_recv.at[turn * PARTS + part],
+            device_id=(tile, first_above if upward else last_below), device_id_type=MESH)
+
+    def send_depth(turn, upward):
+        crosses = crosses_up if upward else crosses_down
+        plain = jnp.logical_and(has_above if upward else has_below, jnp.logical_not(crosses))
+
+        pl.when(plain)(lambda: depth_copy(turn, upward, TX).start())
+
+        @pl.when(crosses)
+        def _():
+            for part in range(PARTS):
+                part_copy(turn, upward, part).start()
+            depth_copy(turn, upward, DIRECT).start()
+
+    def relay_depth(turn):
+        for upward, relays in ((True, relays_up), (False, relays_down)):
+
+            @pl.when(relays)
+            def _():
+                part_copy(turn, upward, 0).wait_recv()
+                relay_copy(turn, upward, relay_part).start()
+
+    def wait_depth(turn):
+        for upward, crosses in ((True, crosses_down), (False, crosses_up)):
+            plain = jnp.logical_and(has_below if upward else has_above, jnp.logical_not(crosses))
+            pl.when(plain)(lambda: depth_copy(turn, upward, TX).wait_recv())
+
+            @pl.when(crosses)
+            def _():
+                depth_copy(turn, upward, DIRECT).wait_recv()
+                for part in range(PARTS):
+                    relay_copy(turn, upward, part).wait_recv()
+
+    def finish_depth(turn):
+        for upward, crosses, relays in ((True, crosses_up, relays_up), (False, crosses_down, relays_down)):
+            plain = jnp.logical_and(has_above if upward else has_below, jnp.logical_not(crosses))
+            pl.when(plain)(lambda: depth_copy(turn, upward, TX).wait_send())
+
+            @pl.when(crosses)
+            def _():
+                for part in range(PARTS):
+                    part_copy(turn, upward, part).wait_send()
+                depth_copy(turn, upward, DIRECT).wait_send()
+
+            pl.when(relays)(lambda: relay_copy(turn, upward, relay_part).wait_send())
 
     def band_copy(kind, group, toward_next):
         first, count = GROUPS[group]
@@ -151,8 +261,8 @@
         for toward_next in (False, True):
             band_copy(kind, group, toward_next).wait_recv()
 
-    loads[0].wait()
-    loads[1].wait()
+    for number in (3, 4, 0, 1):
+        loads[number].wait()
     d0, d1, d2, d3 = (decay[i] for i in range(4))
     c0, c1, c2, c3 = (coupling[i] for i in range(4))
 
@@ -167,8 +277,12 @@
                 put(s0, comp, plane, row, couple * at(field, comp, plane, row))
 
     row_tiles(scale)
-    pl.semaphore_wait(barrier, 4 + has_below.astype(jnp.int32) + has_above.astype(jnp.int32))
-    pl.when(has_below)(lambda: depth_copy(0, False).start())
+    count = lambda flag, number: jnp.where(flag, number, 0)
+    crosses_any = jnp.logical_or(crosses_up, crosses_down)
+    relays_any = jnp.logical_or(relays_up, relays_down)
+    pl.semaphore_wait(
+        barrier, 4 + count(has_below, 1) + count(has_above, 1) + count(crosses_any, 2 * PARTS) + count(relays_any, 2))
+    send_depth(0, False)
     loads[2].wait()
 
     def partial(hbuf, offset, sbuf, abuf):
@@ -180,7 +294,7 @@
         row_tiles(body)
 
     partial(field, HX, s0, a1)
-    pl.when(has_above)(lambda: depth_copy(0, True).start())
+    send_depth(0, True)
 
     def magnetic_local(hbuf, offset, sbuf, row):
         s_x0, s_y0, s_z0 = (at(sbuf, comp, 0, row) for comp in range(3))
@@ -216,10 +330,6 @@
 
             row_tiles(body)
 
-    def wait_depth(turn):
-        pl.when(has_above)(lambda: depth_copy(turn, False).wait_recv())
-        pl.when(has_below)(lambda: depth_copy(turn, True).wait_recv())
-
     def magnetic_rest(turn, abuf, sbuf, row):
         new_x = rows_of(abuf, 0, row) - down_in[turn, 1, pl.ds(row, ROWS), :]
         new_y = rows_of(abuf, 1, row) + down_in[turn, 0, pl.ds(row, ROWS), :]
@@ -239,6 +349,7 @@
         return decays * at(ebuf, 2, plane, row) - MAGNETIC * (minus_x(hbuf, 1, plane, row) - minus_y(h_x))
 
     edge_planes(0, s0)
+    relay_depth(0)
     wait_depth(0)
 
     def first_rest(row):
@@ -254,9 +365,9 @@
                 put(s1, comp, plane, row, couple * new[comp])
 
     row_tiles(first_rest)
-    pl.when(has_below)(lambda: depth_copy(1, False).start())
+    send_depth(1, False)
     partial(h1, 0, s1, a2)
-    pl.when(has_above)(lambda: depth_copy(1, True).start())
+    send_depth(1, True)
 
     def keep(name, row, value, weights):
         w[ORDER.index(name), pl.ds(row, ROWS), :] = value * weights
@@ -275,6 +386,7 @@
         keep((EZ, 0), row, electric_z(e1, h2, 0, row, new_x), weights)
 
     row_tiles(second_local)
+    relay_depth(1)
 
     def slot_of(rows):
         return lax.broadcasted_iota(jnp.int32, (rows, TY), 1) // BAND
@@ -374,29 +486,30 @@
         planes_of(group, add_corners)
         send_band(3, group)
 
-    stores = []
     for group in range(2):
         wait_band(2, group)
         planes_of(group, add_middle)
         wait_band(1, group)
         wait_band(3, group)
         planes_of(group, add_x_bands)
-        first, count = GROUPS[group]
-        for index in range(first, first + count):
-            comp, plane = ORDER[index]
-            store = pltpu.make_async_copy(w.at[index], out.at[0, comp, plane], store_sem.at[index])
-            store.start()
-            stores.append(store)
 
     for turn in range(2):
-        pl.when(has_below)(lambda: depth_copy(turn, False).wait_send())
-        pl.when(has_above)(lambda: depth_copy(turn, True).wait_send())
+        finish_depth(turn)
     for group in range(2):
         for kind in range(4):
             for toward_next in (False, True):
                 band_copy(kind, group, toward_next).wait_send()
-    for store in stores:
-        store.wait()
+
+
+def place(planes, out, sems):
+    copies = [
+        pltpu.make_async_copy(planes.at[index], out.at[0, comp, plane], sems.at[index])
+        for index, (comp, plane) in enumerate(ORDER)
+    ]
+    for copy in copies:
+        copy.start()
+    for copy in copies:
+        copy.wait()
 
 
 def on_device(tiles, subs, seeds, material, decay, coupling):
@@ -404,14 +517,15 @@
     padded = (3, 2, PAD + TX + PAD, TY)
     planes = len(ORDER)
     narrow, wide = pltpu.VMEM((2, planes, 16, TY), f32), pltpu.VMEM((2, planes, 48, TY), f32)
-    smem = pl.BlockSpec(memory_space=pltpu.SMEM)
-    anywhere = pl.BlockSpec(memory_space=pl.ANY)
-    return pl.pallas_call(
+    hbm = pl.BlockSpec(memory_space=pltpu.HBM)
+    done = pl.pallas_call(
         functools.partial(kernel, tiles, subs),
-        out_shape=jax.ShapeDtypeStruct(seeds.shape, f32),
-        in_specs=[smem, smem, anywhere, anywhere],
-        out_specs=anywhere,
+        out_shape=jax.ShapeDtypeStruct((planes, TX, TY), f32),
+        in_specs=[hbm] * 4,
+        out_specs=pl.BlockSpec(memory_space=pltpu.VMEM),
         scratch_shapes=[
+            pltpu.SMEM(decay.shape, f32),
+            pltpu.SMEM(coupling.shape, f32),
             pltpu.VMEM((6, *padded[1:]), f32),
             pltpu.VMEM((2, TX, TY), jnp.int32),
             pltpu.VMEM((2, TX, TY), f32),
@@ -421,18 +535,30 @@
             pltpu.VMEM((2, TX, TY), f32),
             pltpu.VMEM((2, 2, TX, TY), f32),
             pltpu.VMEM((2, 2, TX, TY), f32),
-            pltpu.VMEM((planes, TX, TY), f32),
+            pltpu.VMEM((2, 2, PART_ROWS, TY), f32),
             narrow, wide, narrow, narrow,
             narrow, wide, narrow, narrow,
-            pltpu.SemaphoreType.DMA((3,)),
-            pltpu.SemaphoreType.DMA((planes,)),
+            pltpu.SemaphoreType.DMA((5,)),
             pltpu.SemaphoreType.DMA((4,)),
             pltpu.SemaphoreType.DMA((4,)),
+            pltpu.SemaphoreType.DMA((2 * PARTS,)),
+            pltpu.SemaphoreType.DMA((2 * PARTS,)),
+            pltpu.SemaphoreType.DMA((2,)),
+            pltpu.SemaphoreType.DMA((2,)),
             pltpu.SemaphoreType.DMA((16,)),
             pltpu.SemaphoreType.DMA((16,)),
         ],
-        compiler_params=pltpu.CompilerParams(collective_id=0, has_side_effects=True),
-    )(decay, coupling, seeds, material)
+        compiler_params=pltpu.CompilerParams(
+            collective_id=0, has_side_effects=True, vmem_limit_bytes=20 * 2**20),
+    )(*(pltpu.with_memory_space_constraint(array, pltpu.HBM) for array in (decay, coupling, seeds, material)))
+    return pl.pallas_call(
+        place,
+        out_shape=jax.ShapeDtypeStruct(seeds.shape, f32),
+        in_specs=[pl.BlockSpec(memory_space=pltpu.VMEM)],
+        out_specs=hbm,
+        scratch_shapes=[pltpu.SemaphoreType.DMA((planes,))],
+        compiler_params=pltpu.CompilerParams(vmem_limit_bytes=4 * 2**20),
+    )(done)
 
 
 def solution(mesh):

time: 64.8 us -> 46.3 us (0.71)
  Pallas kernels: 61.9 us -> 46.2 us
  local copies, waits for them, and re-layouts: 2.65 us -> 0 us
    pallas_call x1, Pallas kernels: 61.9 us -> 44.9 us  [on_device(): pl.pallas_call(functools.partial(kernel, tiles, subs), out_shape=jax.Shap...]
    unnamed x1 -> x0, local copies, waits for them, and re-layouts: 2.65 us -> none
    pallas_call x0 -> x1, Pallas kernels: none -> 1.23 us  [on_device(): pl.pallas_call(place, out_shape=jax.ShapeDtypeStruct(seeds.shape, f32), i...]
where the time goes in v2:
time: 46.3 us; the launch traced here: 46.2 us
  Pallas kernels  46.2 us (100%)
    pallas_call x1, Pallas kernels, on_device(): pl.pallas_call(functools.partial(kernel, tiles, subs), out_shape=jax.Shap...  44.9 us
    pallas_call x1, Pallas kernels, on_device(): pl.pallas_call(place, out_shape=jax.ShapeDtypeStruct(seeds.shape, f32), i...  1.23 us

profile of v2, /device:TPU:7, one launch (start us, length us, event | category | flops | bytes accessed | tf_op | source)
XLA Modules:
  0.0 46.2 jit_solution(10888787156641213438)
XLA Ops:
  0.0 44.9 %shard_map.46.planes = f32[12,256,128]{2,1,0:T(8,128)S(1)} custom-call(f32[4]{0:T(128)} %decay_in.1, f32[4]{0:T(128)} %coupling_in.1, f32[1,6,2,256,128]{4,3,2,1,0:T(8,128)} %seeds.1, s32[1,2,256,128]{3,2,1,0:T(8,128)} %material.1), custom_call_target="tpu_custom_call" | custom-call | tf_op jit(solution)/shard_map/pallas_call | solution.py:521
  44.9 1.2 %shard_map.47 = f32[1,6,2,256,128]{4,3,2,1,0:T(8,128)} custom-call(f32[12,256,128]{2,1,0:T(8,128)S(1)} %shard_map.46.planes), custom_call_target="tpu_custom_call" | custom-call | tf_op jit(solution)/shard_map/pallas_call | solution.py:554

commit v3 on v2

--- a/solution.py
+++ b/solution.py
@@ -33,7 +33,7 @@
         body(pl.multiple_of(index * ROWS, ROWS))
         return carry
 
-    lax.fori_loop(0, TX // ROWS, step, 0)
+    lax.fori_loop(0, TX // ROWS, step, 0, unroll=2)
 
 
 def planes_of(group, body):
@@ -43,7 +43,7 @@
         body(index)
         return carry
 
-    lax.fori_loop(first, first + count, step, 0)
+    lax.fori_loop(first, first + count, step, 0, unroll=True)
 
 
 def kernel(
@@ -386,7 +386,6 @@
         keep((EZ, 0), row, electric_z(e1, h2, 0, row, new_x), weights)
 
     row_tiles(second_local)
-    relay_depth(1)
 
     def slot_of(rows):
         return lax.broadcasted_iota(jnp.int32, (rows, TY), 1) // BAND
@@ -461,6 +460,7 @@
         send_band(2, group)
 
     send_group(0)
+    relay_depth(1)
     edge_planes(1, s1)
     wait_depth(1)
 

time: 46.3 us -> 43.9 us (0.948)
  Pallas kernels: 46.2 us -> 43.7 us
    pallas_call x1, Pallas kernels: 44.9 us -> 42.4 us  [on_device(): pl.pallas_call(functools.partial(kernel, tiles, subs), out_shape=jax.Shap...]
where the time goes in v3:
time: 43.9 us; the launch traced here: 43.7 us
  Pallas kernels  43.7 us (100%)
    pallas_call x1, Pallas kernels, on_device(): pl.pallas_call(functools.partial(kernel, tiles, subs), out_shape=jax.Shap...  42.4 us
    pallas_call x1, Pallas kernels, on_device(): pl.pallas_call(place, out_shape=jax.ShapeDtypeStruct(seeds.shape, f32), i...  1.23 us

profile of v3, /device:TPU:7, one launch (start us, length us, event | category | flops | bytes accessed | tf_op | source)
XLA Modules:
  0.0 43.7 jit_solution(6203345468701301302)
XLA Ops:
  0.0 42.4 %shard_map.46.planes = f32[12,256,128]{2,1,0:T(8,128)S(1)} custom-call(f32[4]{0:T(128)} %decay_in.1, f32[4]{0:T(128)} %coupling_in.1, f32[1,6,2,256,128]{4,3,2,1,0:T(8,128)} %seeds.1, s32[1,2,256,128]{3,2,1,0:T(8,128)} %material.1), custom_call_target="tpu_custom_call" | custom-call | tf_op jit(solution)/shard_map/pallas_call | solution.py:521
  42.4 1.2 %shard_map.47 = f32[1,6,2,256,128]{4,3,2,1,0:T(8,128)} custom-call(f32[12,256,128]{2,1,0:T(8,128)S(1)} %shard_map.46.planes), custom_call_target="tpu_custom_call" | custom-call | tf_op jit(solution)/shard_map/pallas_call | solution.py:554

commit v4 on v3

--- a/solution.py
+++ b/solution.py
@@ -27,6 +27,9 @@
 PART_ROWS = 56
 DIRECT = TX - PARTS * PART_ROWS
 
+LINE = 4
+WAYS = (((0, 2), (2, 4), (4, 5)), ((5, 7), (7, 9), (9, 12)))
+
 
 def row_tiles(body):
     def step(index, carry):
@@ -48,9 +51,10 @@
 
 def kernel(
     tiles, subs, decay_in, coupling_in, seeds, material, w,
-    decay, coupling, field, mat, ca, cb, s0, s1, h1, h2, e1, a1, a2, up_in, down_in, relay_in,
+    decay, coupling, field, mat, ca, cb, s0, s1, h1, h2, e1, a1, a2, up_in, down_in, relay_in, xr_in,
     yc_out, yn_out, xn_out, xc_out, yc_in, yn_in, xn_in, xc_in,
     load_sem, depth_send, depth_recv, part_send, part_recv, relay_recv, relay_send, band_send, band_recv,
+    way_send, way_recv, pass_send, pass_recv,
 ):
     tile = lax.axis_index("tile")
     sub = lax.axis_index("sub")
@@ -103,6 +107,33 @@
     def down_relay(part):
         return start + 2 * part + 2
 
+    in_line = lax.rem(tile, LINE)
+
+    def tile_at(distance):
+        return lax.rem(tile + tiles + distance, tiles)
+
+    def sends_around(direction):
+        return in_line == (LINE - 1 if direction else 0)
+
+    def gets_around(direction):
+        return in_line == (0 if direction else LINE - 1)
+
+    def passes_on(direction, way):
+        return in_line == (way if direction else LINE - 1 - way)
+
+    for direction in range(2):
+        sign = 1 if direction else -1
+        for way in range(1, LINE):
+            pl.when(sends_around(direction))(lambda: greet(tile_at(sign * (1 + way)), sub))
+            pl.when(gets_around(direction))(lambda: greet(tile_at(sign * way), sub))
+
+            @pl.when(passes_on(direction, way))
+            def _():
+                greet(tile_at(-sign * (1 + way)), sub)
+                greet(tile_at(-sign * way), sub)
+
+    ends_line = jnp.logical_or(in_line == 0, in_line == LINE - 1)
+
     @pl.when(crosses_up)
     def _():
         for part in range(PARTS):
@@ -253,13 +284,59 @@
             band_send.at[slot], band_recv.at[slot],
             device_id=(other, sub), device_id_type=MESH)
 
+    def way_slot(group, direction, way):
+        return (group * 2 + direction) * (LINE - 1) + way - 1
+
+    def way_copy(group, direction, way):
+        part = slice(*WAYS[group][way - 1])
+        sign = 1 if direction else -1
+        return pltpu.make_async_remote_copy(
+            xn_out.at[direction, part], xr_in.at[direction, part],
+            way_send.at[way_slot(group, direction, way)], way_recv.at[group * 2 + direction],
+            device_id=(tile_at(sign * (1 + way)), sub), device_id_type=MESH)
+
+    def pass_copy(group, direction, way):
+        part = slice(*WAYS[group][way - 1])
+        sign = 1 if direction else -1
+        return pltpu.make_async_remote_copy(
+            xr_in.at[direction, part], xn_in.at[direction, part],
+            pass_send.at[group * 2 + direction], pass_recv.at[way_slot(group, direction, way)],
+            device_id=(tile_at(-sign * way), sub), device_id_type=MESH)
+
+    def each_band(kind, group, role, straight, around):
+        for direction in (0, 1):
+            if kind != 1:
+                straight(band_copy(kind, group, direction))
+                continue
+            pl.when(jnp.logical_not(role(direction)))(lambda: straight(band_copy(kind, group, direction)))
+
+            @pl.when(role(direction))
+            def _():
+                for way in range(1, LINE):
+                    around(group, direction, way)
+
     def send_band(kind, group):
-        for toward_next in (False, True):
-            band_copy(kind, group, toward_next).start()
+        each_band(kind, group, sends_around, lambda copy: copy.start(), lambda *at: way_copy(*at).start())
 
     def wait_band(kind, group):
-        for toward_next in (False, True):
-            band_copy(kind, group, toward_next).wait_recv()
+        each_band(kind, group, gets_around, lambda copy: copy.wait_recv(), lambda *at: pass_copy(*at).wait_recv())
+
+    def finish_band(kind, group):
+        each_band(kind, group, sends_around, lambda copy: copy.wait_send(), lambda *at: way_copy(*at).wait_send())
+
+    def pass_bands(group):
+        for direction in range(2):
+            for way in range(1, LINE):
+
+                @pl.when(passes_on(direction, way))
+                def _():
+                    way_copy(group, direction, way).wait_recv()
+                    pass_copy(group, direction, way).start()
+
+    def finish_passing(group):
+        for direction in range(2):
+            for way in range(1, LINE):
+                pl.when(passes_on(direction, way))(lambda: pass_copy(group, direction, way).wait_send())
 
     for number in (3, 4, 0, 1):
         loads[number].wait()
@@ -281,7 +358,7 @@
     crosses_any = jnp.logical_or(crosses_up, crosses_down)
     relays_any = jnp.logical_or(relays_up, relays_down)
     pl.semaphore_wait(
-        barrier, 4 + count(has_below, 1) + count(has_above, 1) + count(crosses_any, 2 * PARTS) + count(relays_any, 2))
+        barrier, 4 + jnp.where(ends_line, 8, 4) + count(has_below, 1) + count(has_above, 1) + count(crosses_any, 2 * PARTS) + count(relays_any, 2))
     send_depth(0, False)
     loads[2].wait()
 
@@ -482,6 +559,7 @@
     send_group(1)
 
     for group in range(2):
+        pass_bands(group)
         wait_band(0, group)
         planes_of(group, add_corners)
         send_band(3, group)
@@ -497,8 +575,8 @@
         finish_depth(turn)
     for group in range(2):
         for kind in range(4):
-            for toward_next in (False, True):
-                band_copy(kind, group, toward_next).wait_send()
+            finish_band(kind, group)
+        finish_passing(group)
 
 
 def place(planes, out, sems):
@@ -536,6 +614,7 @@
             pltpu.VMEM((2, 2, TX, TY), f32),
             pltpu.VMEM((2, 2, TX, TY), f32),
             pltpu.VMEM((2, 2, PART_ROWS, TY), f32),
+            narrow,
             narrow, wide, narrow, narrow,
             narrow, wide, narrow, narrow,
             pltpu.SemaphoreType.DMA((5,)),
@@ -547,6 +626,10 @@
             pltpu.SemaphoreType.DMA((2,)),
             pltpu.SemaphoreType.DMA((16,)),
             pltpu.SemaphoreType.DMA((16,)),
+            pltpu.SemaphoreType.DMA((4 * (LINE - 1),)),
+            pltpu.SemaphoreType.DMA((4,)),
+            pltpu.SemaphoreType.DMA((4,)),
+            pltpu.SemaphoreType.DMA((4 * (LINE - 1),)),
         ],
         compiler_params=pltpu.CompilerParams(
             collective_id=0, has_side_effects=True, vmem_limit_bytes=20 * 2**20),

time: 43.9 us -> 44.8 us (1.021)
  Pallas kernels: 43.7 us -> 44.6 us
    pallas_call x1, Pallas kernels: 42.4 us -> 43.4 us  [on_device(): pl.pallas_call(functools.partial(kernel, tiles, subs), out_shape=jax.Shap...]
where the time goes in v4:
time: 44.8 us; the launch traced here: 44.6 us
  Pallas kernels  44.6 us (100%)
    pallas_call x1, Pallas kernels, on_device(): pl.pallas_call(functools.partial(kernel, tiles, subs), out_shape=jax.Shap...  43.4 us
    pallas_call x1, Pallas kernels, on_device(): pl.pallas_call(place, out_shape=jax.ShapeDtypeStruct(seeds.shape, f32), i...  1.23 us

profile of v4, /device:TPU:7, one launch (start us, length us, event | category | flops | bytes accessed | tf_op | source)
XLA Modules:
  0.0 44.6 jit_solution(2484485214604365495)
XLA Ops:
  0.0 43.4 %shard_map.46.planes = f32[12,256,128]{2,1,0:T(8,128)S(1)} custom-call(f32[4]{0:T(128)} %decay_in.1, f32[4]{0:T(128)} %coupling_in.1, f32[1,6,2,256,128]{4,3,2,1,0:T(8,128)} %seeds.1, s32[1,2,256,128]{3,2,1,0:T(8,128)} %material.1), custom_call_target="tpu_custom_call" | custom-call | tf_op jit(solution)/shard_map/pallas_call | solution.py:599
  43.4 1.2 %shard_map.47 = f32[1,6,2,256,128]{4,3,2,1,0:T(8,128)} custom-call(f32[12,256,128]{2,1,0:T(8,128)S(1)} %shard_map.46.planes), custom_call_target="tpu_custom_call" | custom-call | tf_op jit(solution)/shard_map/pallas_call | solution.py:637

commit v5 on v3

--- a/solution.py
+++ b/solution.py
@@ -24,8 +24,9 @@
 
 RUN = 8
 PARTS = 3
-PART_ROWS = 56
-DIRECT = TX - PARTS * PART_ROWS
+DIRECT = 104
+PIECES = (((104, 40), (144, 40), (184, 72)), ((104, 72), (176, 40), (216, 40)))
+MOST = 72
 
 
 def row_tiles(body):
@@ -48,7 +49,8 @@
 
 def kernel(
     tiles, subs, decay_in, coupling_in, seeds, material, w,
-    decay, coupling, field, mat, ca, cb, s0, s1, h1, h2, e1, a1, a2, up_in, down_in, relay_in,
+    decay, coupling, field, mat, ca, cb, s0, s1, h1, h2, e1, decayed, under, mixed,
+    up_out0, up_out1, down_out0, down_out1, up_in0, up_in1, down_in0, down_in1, relay_in0, relay_in1,
     yc_out, yn_out, xn_out, xc_out, yc_in, yn_in, xn_in, xc_in,
     load_sem, depth_send, depth_recv, part_send, part_recv, relay_recv, relay_send, band_send, band_recv,
 ):
@@ -92,7 +94,10 @@
     odd = lax.rem(place_in_run, 2) == 1
     relays_up = jnp.logical_and(jnp.logical_and(odd, place_in_run < RUN - 1), run_above)
     relays_down = jnp.logical_and(jnp.logical_and(jnp.logical_not(odd), place_in_run > 0), run_below)
-    relay_part = jnp.where(odd, place_in_run // 2, jnp.maximum(place_in_run // 2 - 1, 0))
+
+    def relays(upward, part):
+        return jnp.logical_and(place_in_run == 2 * part + (1 if upward else 2), run_above if upward else run_below)
+
     last_here = start + RUN - 1
     first_above = jnp.minimum(start + RUN, subs - 1)
     last_below = jnp.maximum(start - 1, 0)
@@ -135,6 +140,11 @@
                 buf[comp, plane, PAD + TX : PAD + TX + PAD, :] = zeros_pad
             for buf in (h1, h2):
                 buf[comp, plane, 0:PAD, :] = zeros_pad
+    for buf in (decayed, mixed):
+        buf[0, 0, PAD + TX : PAD + TX + PAD, :] = zeros_pad
+    under[1, 0, 0:PAD, :] = zeros_pad
+    up_out, down_out = (up_out0, up_out1), (down_out0, down_out1)
+    up_in, down_in, relay_in = (up_in0, up_in1), (down_in0, down_in1), (relay_in0, relay_in1)
 
     def at(buf, comp, plane, row):
         return buf[comp, plane, pl.ds(PAD + row, ROWS), :]
@@ -169,29 +179,28 @@
         return buf[index, pl.ds(row, ROWS), :]
 
     def depth_rows(turn, upward, first, count):
-        if upward:
-            return (a1, a2)[turn].at[:, first : first + count]
-        return (s0, s1)[turn].at[0:2, 0, PAD + first : PAD + first + count]
+        return (up_out if upward else down_out)[turn].at[:, first : first + count]
 
     def depth_copy(turn, upward, count):
         slot = turn * 2 + int(upward)
         return pltpu.make_async_remote_copy(
-            depth_rows(turn, upward, 0, count), (up_in if upward else down_in).at[turn, :, 0:count],
+            depth_rows(turn, upward, 0, count), (up_in if upward else down_in)[turn].at[:, 0:count],
             depth_send.at[slot], depth_recv.at[slot],
             device_id=(tile, above if upward else below), device_id_type=MESH)
 
     def part_copy(turn, upward, part):
         relay = up_relay(part) if upward else down_relay(part)
+        first, count = PIECES[int(upward)][part]
         return pltpu.make_async_remote_copy(
-            depth_rows(turn, upward, DIRECT + part * PART_ROWS, PART_ROWS), relay_in.at[turn],
+            depth_rows(turn, upward, first, count), relay_in[turn].at[:, 0:count],
             part_send.at[turn * PARTS + part], relay_recv.at[turn],
             device_id=(tile, relay), device_id_type=MESH)
 
     def relay_copy(turn, upward, part):
-        target = (up_in if upward else down_in).at[
-            turn, :, pl.ds(pl.multiple_of(DIRECT + part * PART_ROWS, 8), PART_ROWS)]
+        first, count = PIECES[int(upward)][part]
         return pltpu.make_async_remote_copy(
-            relay_in.at[turn], target, relay_send.at[turn], part_recv.at[turn * PARTS + part],
+            relay_in[turn].at[:, 0:count], (up_in if upward else down_in)[turn].at[:, first : first + count],
+            relay_send.at[turn], part_recv.at[turn * PARTS + part],
             device_id=(tile, first_above if upward else last_below), device_id_type=MESH)
 
     def send_depth(turn, upward):
@@ -202,17 +211,18 @@
 
         @pl.when(crosses)
         def _():
-            for part in range(PARTS):
+            for part in (1, 0, 2) if not upward else (1, 2, 0):
                 part_copy(turn, upward, part).start()
             depth_copy(turn, upward, DIRECT).start()
 
     def relay_depth(turn):
-        for upward, relays in ((True, relays_up), (False, relays_down)):
-
-            @pl.when(relays)
-            def _():
-                part_copy(turn, upward, 0).wait_recv()
-                relay_copy(turn, upward, relay_part).start()
+        for upward in (True, False):
+            for part in range(PARTS):
+
+                @pl.when(relays(upward, part))
+                def _():
+                    part_copy(turn, upward, part).wait_recv()
+                    relay_copy(turn, upward, part).start()
 
     def wait_depth(turn):
         for upward, crosses in ((True, crosses_down), (False, crosses_up)):
@@ -226,7 +236,7 @@
                     relay_copy(turn, upward, part).wait_recv()
 
     def finish_depth(turn):
-        for upward, crosses, relays in ((True, crosses_up, relays_up), (False, crosses_down, relays_down)):
+        for upward, crosses in ((True, crosses_up), (False, crosses_down)):
             plain = jnp.logical_and(has_above if upward else has_below, jnp.logical_not(crosses))
             pl.when(plain)(lambda: depth_copy(turn, upward, TX).wait_send())
 
@@ -236,7 +246,8 @@
                     part_copy(turn, upward, part).wait_send()
                 depth_copy(turn, upward, DIRECT).wait_send()
 
-            pl.when(relays)(lambda: relay_copy(turn, upward, relay_part).wait_send())
+            for part in range(PARTS):
+                pl.when(relays(upward, part))(lambda: relay_copy(turn, upward, part).wait_send())
 
     def band_copy(kind, group, toward_next):
         first, count = GROUPS[group]
@@ -271,10 +282,18 @@
             label = mat[plane, pl.ds(row, ROWS), :]
             is0, is1, is2 = label == 0, label == 1, label == 2
             couple = jnp.where(is0, c0, jnp.where(is1, c1, jnp.where(is2, c2, c3)))
+            decays = jnp.where(is0, d0, jnp.where(is1, d1, jnp.where(is2, d2, d3)))
             cb[plane, pl.ds(row, ROWS), :] = couple
-            ca[plane, pl.ds(row, ROWS), :] = jnp.where(is0, d0, jnp.where(is1, d1, jnp.where(is2, d2, d3)))
+            ca[plane, pl.ds(row, ROWS), :] = decays
+            (down_out, up_out)[plane][1][2, pl.ds(row, ROWS), :] = couple
+            scaled = [couple * at(field, comp, plane, row) for comp in range(3)]
             for comp in range(3):
-                put(s0, comp, plane, row, couple * at(field, comp, plane, row))
+                put(s0, comp, plane, row, scaled[comp])
+            if plane == 0:
+                for comp in range(2):
+                    down_out[0][comp, pl.ds(row, ROWS), :] = scaled[comp]
+            else:
+                put(decayed, 0, 0, row, decays * scaled[2])
 
     row_tiles(scale)
     count = lambda flag, number: jnp.where(flag, number, 0)
@@ -285,15 +304,16 @@
     send_depth(0, False)
     loads[2].wait()
 
-    def partial(hbuf, offset, sbuf, abuf):
-        def body(row):
-            s_x, s_y, s_z = (at(sbuf, comp, 1, row) for comp in range(3))
-            abuf[0, pl.ds(row, ROWS), :] = at(hbuf, offset, 1, row) + plus_y(s_z) + s_y
-            abuf[1, pl.ds(row, ROWS), :] = at(hbuf, offset + 1, 1, row) - s_x - plus_x(sbuf, 2, 1, row)
-
-        row_tiles(body)
-
-    partial(field, HX, s0, a1)
+    def without_above(hbuf, offset, sbuf, row):
+        s_x, s_y, s_z = (at(sbuf, comp, 1, row) for comp in range(3))
+        part_x = at(hbuf, offset, 1, row) + plus_y(s_z) + s_y
+        part_y = at(hbuf, offset + 1, 1, row) - s_x - plus_x(sbuf, 2, 1, row)
+        return part_x, part_y
+
+    def first_partial(row):
+        up_out[0][0, pl.ds(row, ROWS), :], up_out[0][1, pl.ds(row, ROWS), :] = without_above(field, HX, s0, row)
+
+    row_tiles(first_partial)
     send_depth(0, True)
 
     def magnetic_local(hbuf, offset, sbuf, row):
@@ -313,29 +333,41 @@
 
     row_tiles(first_local)
 
-    def edge_planes(turn, sbuf):
-        @pl.when(jnp.logical_not(has_above))
-        def _():
-            def body(row):
-                for comp in range(2):
-                    down_in[turn, comp, pl.ds(row, ROWS), :] = jnp.zeros((ROWS, TY), jnp.float32)
-
-            row_tiles(body)
-
-        @pl.when(jnp.logical_not(has_below))
-        def _():
-            def body(row):
-                up_in[turn, 0, pl.ds(row, ROWS), :] = at(sbuf, 1, 0, row)
-                up_in[turn, 1, pl.ds(row, ROWS), :] = -at(sbuf, 0, 0, row)
-
-            row_tiles(body)
-
-    def magnetic_rest(turn, abuf, sbuf, row):
-        new_x = rows_of(abuf, 0, row) - down_in[turn, 1, pl.ds(row, ROWS), :]
-        new_y = rows_of(abuf, 1, row) + down_in[turn, 0, pl.ds(row, ROWS), :]
-        under_x = up_in[turn, 0, pl.ds(row, ROWS), :] - at(sbuf, 1, 0, row)
-        under_y = up_in[turn, 1, pl.ds(row, ROWS), :] + at(sbuf, 0, 0, row)
-        return new_x, new_y, under_x, under_y
+    def second_terms(row):
+        h_x, h_y = at(h1, 0, 0, row), at(h1, 1, 0, row)
+        decays, couple = rows_of(ca, 1, row), rows_of(cb, 1, row)
+        part_x = decays * at(field, EX, 1, row) - MAGNETIC * (minus_y(at(h1, 2, 1, row)) + h_y)
+        part_y = decays * at(field, EY, 1, row) + MAGNETIC * (h_x + minus_x(h1, 2, 1, row))
+        up_out[1][0, pl.ds(row, ROWS), :] = plus_y(at(decayed, 0, 0, row)) + couple * part_y
+        up_out[1][1, pl.ds(row, ROWS), :] = -couple * part_x - plus_x(decayed, 0, 0, row)
+        decays, couple = rows_of(ca, 0, row), rows_of(cb, 0, row)
+        down_out[1][0, pl.ds(row, ROWS), :] = couple * (
+            decays * at(field, EX, 0, row) - MAGNETIC * (minus_y(at(h1, 2, 0, row)) - h_y))
+        down_out[1][1, pl.ds(row, ROWS), :] = couple * (
+            decays * at(field, EY, 0, row) - MAGNETIC * (h_x - minus_x(h1, 2, 0, row)))
+
+    row_tiles(second_terms)
+    send_depth(1, False)
+    send_depth(1, True)
+
+    @pl.when(jnp.logical_not(has_above))
+    def _():
+        def clear(row):
+            for buf in down_in:
+                for comp in range(buf.shape[0]):
+                    buf[comp, pl.ds(row, ROWS), :] = jnp.zeros((ROWS, TY), jnp.float32)
+
+        row_tiles(clear)
+
+    @pl.when(jnp.logical_not(has_below))
+    def _():
+        def cancel(row):
+            up_in[0][0, pl.ds(row, ROWS), :] = at(s0, 1, 0, row)
+            up_in[0][1, pl.ds(row, ROWS), :] = -at(s0, 0, 0, row)
+            for comp in range(3):
+                up_in[1][comp, pl.ds(row, ROWS), :] = jnp.zeros((ROWS, TY), jnp.float32)
+
+        row_tiles(cancel)
 
     def electric_xy(ebuf, hbuf, plane, row, h_x, h_y, under_x, under_y):
         h_z = at(hbuf, 2, plane, row)
@@ -348,14 +380,19 @@
         decays = rows_of(ca, plane, row)
         return decays * at(ebuf, 2, plane, row) - MAGNETIC * (minus_x(hbuf, 1, plane, row) - minus_y(h_x))
 
-    edge_planes(0, s0)
     relay_depth(0)
     wait_depth(0)
+    relay_depth(1)
 
     def first_rest(row):
-        x1, y1, under_x, under_y = magnetic_rest(0, a1, s0, row)
+        x1 = rows_of(up_out[0], 0, row) - rows_of(down_in[0], 1, row)
+        y1 = rows_of(up_out[0], 1, row) + rows_of(down_in[0], 0, row)
+        under_x = rows_of(up_in[0], 0, row) - at(s0, 1, 0, row)
+        under_y = rows_of(up_in[0], 1, row) + at(s0, 0, 0, row)
         put(h1, 0, 1, row, x1)
         put(h1, 1, 1, row, y1)
+        put(under, 0, 0, row, under_x)
+        put(under, 1, 0, row, under_y)
         x0, y0 = at(h1, 0, 0, row), at(h1, 1, 0, row)
         for plane, (h_x, h_y, b_x, b_y) in enumerate(((x0, y0, under_x, under_y), (x1, y1, x0, y0))):
             new = (*electric_xy(field, h1, plane, row, h_x, h_y, b_x, b_y), electric_z(field, h1, plane, row, h_x))
@@ -365,9 +402,6 @@
                 put(s1, comp, plane, row, couple * new[comp])
 
     row_tiles(first_rest)
-    send_depth(1, False)
-    partial(h1, 0, s1, a2)
-    send_depth(1, True)
 
     def keep(name, row, value, weights):
         w[ORDER.index(name), pl.ds(row, ROWS), :] = value * weights
@@ -460,12 +494,25 @@
         send_band(2, group)
 
     send_group(0)
-    relay_depth(1)
-    edge_planes(1, s1)
     wait_depth(1)
 
+    def mix(row):
+        turn_z = minus_x(under, 1, 0, row) - minus_y(at(under, 0, 0, row))
+        put(mixed, 0, 0, row, MAGNETIC * rows_of(up_in[1], 2, row) * turn_z)
+
+    row_tiles(mix)
+
     def second_rest(row):
-        x1, y1, under_x, under_y = magnetic_rest(1, a2, s1, row)
+        x1, y1 = without_above(h1, 0, s1, row)
+        couple = MAGNETIC * rows_of(down_in[1], 2, row)
+        x1 -= rows_of(down_in[1], 1, row) + couple * at(h1, 0, 1, row)
+        y1 += rows_of(down_in[1], 0, row) - couple * at(h1, 1, 1, row)
+        couple = MAGNETIC * rows_of(up_in[1], 2, row)
+        under_x, under_y = at(under, 0, 0, row), at(under, 1, 0, row)
+        under_x += rows_of(up_in[1], 0, row) - couple * under_x - plus_y(at(mixed, 0, 0, row)) - at(s1, 1, 0, row)
+        under_y += rows_of(up_in[1], 1, row) - couple * under_y + plus_x(mixed, 0, 0, row) + at(s1, 0, 0, row)
+        under_x = jnp.where(has_below, under_x, 0.0)
+        under_y = jnp.where(has_below, under_y, 0.0)
         put(h2, 0, 1, row, x1)
         put(h2, 1, 1, row, y1)
         x0, y0 = at(h2, 0, 0, row), at(h2, 1, 0, row)
@@ -531,11 +578,9 @@
             pltpu.VMEM((2, TX, TY), f32),
             pltpu.VMEM((2, TX, TY), f32),
             *[pltpu.VMEM(padded, f32)] * 5,
-            pltpu.VMEM((2, TX, TY), f32),
-            pltpu.VMEM((2, TX, TY), f32),
-            pltpu.VMEM((2, 2, TX, TY), f32),
-            pltpu.VMEM((2, 2, TX, TY), f32),
-            pltpu.VMEM((2, 2, PART_ROWS, TY), f32),
+            *[pltpu.VMEM((count, 1, *padded[2:]), f32) for count in (1, 2, 1)],
+            *[pltpu.VMEM((count, TX, TY), f32) for count in (2, 3)] * 4,
+            *[pltpu.VMEM((count, MOST, TY), f32) for count in (2, 3)],
             narrow, wide, narrow, narrow,
             narrow, wide, narrow, narrow,
             pltpu.SemaphoreType.DMA((5,)),

time: 43.9 us -> 38.6 us (0.88)
  Pallas kernels: 43.7 us -> 38.3 us
    pallas_call x1, Pallas kernels: 42.4 us -> 37.1 us  [on_device(): pl.pallas_call(functools.partial(kernel, tiles, subs), out_shape=jax.Shap...]
where the time goes in v5:
time: 38.6 us; the launch traced here: 38.3 us
  Pallas kernels  38.3 us (99%)
    pallas_call x1, Pallas kernels, on_device(): pl.pallas_call(functools.partial(kernel, tiles, subs), out_shape=jax.Shap...  37.1 us
    pallas_call x1, Pallas kernels, on_device(): pl.pallas_call(place, out_shape=jax.ShapeDtypeStruct(seeds.shape, f32), i...  1.23 us

profile of v5, /device:TPU:7, one launch (start us, length us, event | category | flops | bytes accessed | tf_op | source)
XLA Modules:
  0.0 38.3 jit_solution(1266071741282817087)
XLA Ops:
  0.0 37.1 %shard_map.46.planes = f32[12,256,128]{2,1,0:T(8,128)S(1)} custom-call(f32[4]{0:T(128)} %decay_in.1, f32[4]{0:T(128)} %coupling_in.1, f32[1,6,2,256,128]{4,3,2,1,0:T(8,128)} %seeds.1, s32[1,2,256,128]{3,2,1,0:T(8,128)} %material.1), custom_call_target="tpu_custom_call" | custom-call | tf_op jit(solution)/shard_map/pallas_call | solution.py:568
  37.1 1.2 %shard_map.47 = f32[1,6,2,256,128]{4,3,2,1,0:T(8,128)} custom-call(f32[12,256,128]{2,1,0:T(8,128)S(1)} %shard_map.46.planes), custom_call_target="tpu_custom_call" | custom-call | tf_op jit(solution)/shard_map/pallas_call | solution.py:599

commit v6 on v5

--- a/solution.py
+++ b/solution.py
@@ -81,19 +81,16 @@
     def greet(other_tile, other_sub):
         pl.semaphore_signal(barrier, inc=1, device_id=(other_tile, other_sub), device_id_type=MESH)
 
+    pl.when(has_below)(lambda: greet(tile, below))
+    pl.when(has_above)(lambda: greet(tile, above))
     for other in (x_prev, x_next, y_prev, y_next):
         greet(other, sub)
-    pl.when(has_below)(lambda: greet(tile, below))
-    pl.when(has_above)(lambda: greet(tile, above))
     place_in_run = lax.rem(sub, RUN)
     start = sub - place_in_run
     run_above = start + RUN < subs
     run_below = start > 0
     crosses_up = jnp.logical_and(place_in_run == RUN - 1, run_above)
     crosses_down = jnp.logical_and(place_in_run == 0, run_below)
-    odd = lax.rem(place_in_run, 2) == 1
-    relays_up = jnp.logical_and(jnp.logical_and(odd, place_in_run < RUN - 1), run_above)
-    relays_down = jnp.logical_and(jnp.logical_and(jnp.logical_not(odd), place_in_run > 0), run_below)
 
     def relays(upward, part):
         return jnp.logical_and(place_in_run == 2 * part + (1 if upward else 2), run_above if upward else run_below)
@@ -108,27 +105,9 @@
     def down_relay(part):
         return start + 2 * part + 2
 
-    @pl.when(crosses_up)
-    def _():
-        for part in range(PARTS):
-            greet(tile, up_relay(part))
-            greet(tile, jnp.minimum(down_relay(part) + RUN, subs - 1))
-
-    @pl.when(crosses_down)
-    def _():
-        for part in range(PARTS):
-            greet(tile, down_relay(part))
-            greet(tile, jnp.maximum(up_relay(part) - RUN, 0))
-
-    @pl.when(relays_up)
-    def _():
-        greet(tile, last_here)
-        greet(tile, first_above)
-
-    @pl.when(relays_down)
-    def _():
-        greet(tile, start)
-        greet(tile, last_below)
+    for part in range(PARTS):
+        pl.when(relays(True, part))(lambda: greet(tile, last_here))
+        pl.when(relays(False, part))(lambda: greet(tile, start))
 
     lane = lax.broadcasted_iota(jnp.int32, (ROWS, TY), 1)
     not_last = lane < TY - 1
@@ -215,11 +194,18 @@
                 part_copy(turn, upward, part).start()
             depth_copy(turn, upward, DIRECT).start()
 
-    def relay_depth(turn):
+    late_up = start == 0
+
+    def relay_depth(turn, late):
         for upward in (True, False):
+            if late and not upward:
+                continue
             for part in range(PARTS):
-
-                @pl.when(relays(upward, part))
+                now = relays(upward, part)
+                if upward:
+                    now = jnp.logical_and(now, late_up if late else jnp.logical_not(late_up))
+
+                @pl.when(now)
                 def _():
                     part_copy(turn, upward, part).wait_recv()
                     relay_copy(turn, upward, part).start()
@@ -298,9 +284,7 @@
     row_tiles(scale)
     count = lambda flag, number: jnp.where(flag, number, 0)
     crosses_any = jnp.logical_or(crosses_up, crosses_down)
-    relays_any = jnp.logical_or(relays_up, relays_down)
-    pl.semaphore_wait(
-        barrier, 4 + count(has_below, 1) + count(has_above, 1) + count(crosses_any, 2 * PARTS) + count(relays_any, 2))
+    pl.semaphore_wait(barrier, 4 + count(has_below, 1) + count(has_above, 1) + count(crosses_any, PARTS))
     send_depth(0, False)
     loads[2].wait()
 
@@ -380,9 +364,9 @@
         decays = rows_of(ca, plane, row)
         return decays * at(ebuf, 2, plane, row) - MAGNETIC * (minus_x(hbuf, 1, plane, row) - minus_y(h_x))
 
-    relay_depth(0)
+    relay_depth(0, False)
     wait_depth(0)
-    relay_depth(1)
+    relay_depth(1, False)
 
     def first_rest(row):
         x1 = rows_of(up_out[0], 0, row) - rows_of(down_in[0], 1, row)
@@ -494,6 +478,8 @@
         send_band(2, group)
 
     send_group(0)
+    relay_depth(0, True)
+    relay_depth(1, True)
     wait_depth(1)
 
     def mix(row):

time: 38.6 us -> 37.5 us (0.972)
  Pallas kernels: 38.3 us -> 37.4 us
    pallas_call x1, Pallas kernels: 37.1 us -> 36.2 us  [on_device(): pl.pallas_call(functools.partial(kernel, tiles, subs), out_shape=jax.Shap...]
where the time goes in v6:
time: 37.5 us; the launch traced here: 37.4 us
  Pallas kernels  37.4 us (100%)
    pallas_call x1, Pallas kernels, on_device(): pl.pallas_call(functools.partial(kernel, tiles, subs), out_shape=jax.Shap...  36.2 us
    pallas_call x1, Pallas kernels, on_device(): pl.pallas_call(place, out_shape=jax.ShapeDtypeStruct(seeds.shape, f32), i...  1.23 us

profile of v6, /device:TPU:7, one launch (start us, length us, event | category | flops | bytes accessed | tf_op | source)
XLA Modules:
  0.0 37.4 jit_solution(3299097638945216544)
XLA Ops:
  0.0 36.2 %shard_map.46.planes = f32[12,256,128]{2,1,0:T(8,128)S(1)} custom-call(f32[4]{0:T(128)} %decay_in.1, f32[4]{0:T(128)} %coupling_in.1, f32[1,6,2,256,128]{4,3,2,1,0:T(8,128)} %seeds.1, s32[1,2,256,128]{3,2,1,0:T(8,128)} %material.1), custom_call_target="tpu_custom_call" | custom-call | tf_op jit(solution)/shard_map/pallas_call | solution.py:554
  36.2 1.2 %shard_map.47 = f32[1,6,2,256,128]{4,3,2,1,0:T(8,128)} custom-call(f32[12,256,128]{2,1,0:T(8,128)S(1)} %shard_map.46.planes), custom_call_target="tpu_custom_call" | custom-call | tf_op jit(solution)/shard_map/pallas_call | solution.py:585

commit v7 on v6

--- a/solution.py
+++ b/solution.py
@@ -18,9 +18,10 @@
 EX, EY, EZ, HX, HY, HZ = range(6)
 
 EARLY = ((HX, 0), (HY, 0), (HZ, 0), (HZ, 1), (EZ, 0))
-LATE = ((HX, 1), (HY, 1), (EX, 0), (EY, 0), (EX, 1), (EY, 1), (EZ, 1))
-ORDER = EARLY + LATE
-GROUPS = ((0, len(EARLY)), (len(EARLY), len(LATE)))
+UPPER = ((HX, 1), (HY, 1), (EX, 1), (EY, 1), (EZ, 1))
+LOWER = ((EX, 0), (EY, 0))
+ORDER = EARLY + UPPER + LOWER
+GROUPS = ((0, 5), (5, 5), (10, 2))
 
 RUN = 8
 PARTS = 3
@@ -210,16 +211,16 @@
                     part_copy(turn, upward, part).wait_recv()
                     relay_copy(turn, upward, part).start()
 
-    def wait_depth(turn):
-        for upward, crosses in ((True, crosses_down), (False, crosses_up)):
-            plain = jnp.logical_and(has_below if upward else has_above, jnp.logical_not(crosses))
-            pl.when(plain)(lambda: depth_copy(turn, upward, TX).wait_recv())
-
-            @pl.when(crosses)
-            def _():
-                depth_copy(turn, upward, DIRECT).wait_recv()
-                for part in range(PARTS):
-                    relay_copy(turn, upward, part).wait_recv()
+    def wait_depth(turn, upward):
+        crosses = crosses_down if upward else crosses_up
+        plain = jnp.logical_and(has_below if upward else has_above, jnp.logical_not(crosses))
+        pl.when(plain)(lambda: depth_copy(turn, upward, TX).wait_recv())
+
+        @pl.when(crosses)
+        def _():
+            depth_copy(turn, upward, DIRECT).wait_recv()
+            for part in range(PARTS):
+                relay_copy(turn, upward, part).wait_recv()
 
     def finish_depth(turn):
         for upward, crosses in ((True, crosses_up), (False, crosses_down)):
@@ -243,7 +244,7 @@
             other = y_next if toward_next else y_prev
         else:
             other = x_next if toward_next else x_prev
-        slot = (kind * 2 + group) * 2 + direction
+        slot = (kind * len(GROUPS) + group) * 2 + direction
         part = slice(first, first + count)
         return pltpu.make_async_remote_copy(
             source.at[direction, part], target.at[direction, part],
@@ -365,7 +366,8 @@
         return decays * at(ebuf, 2, plane, row) - MAGNETIC * (minus_x(hbuf, 1, plane, row) - minus_y(h_x))
 
     relay_depth(0, False)
-    wait_depth(0)
+    wait_depth(0, True)
+    wait_depth(0, False)
     relay_depth(1, False)
 
     def first_rest(row):
@@ -480,46 +482,72 @@
     send_group(0)
     relay_depth(0, True)
     relay_depth(1, True)
-    wait_depth(1)
-
-    def mix(row):
-        turn_z = minus_x(under, 1, 0, row) - minus_y(at(under, 0, 0, row))
-        put(mixed, 0, 0, row, MAGNETIC * rows_of(up_in[1], 2, row) * turn_z)
-
-    row_tiles(mix)
-
-    def second_rest(row):
+    def upper_rows(row):
         x1, y1 = without_above(h1, 0, s1, row)
         couple = MAGNETIC * rows_of(down_in[1], 2, row)
         x1 -= rows_of(down_in[1], 1, row) + couple * at(h1, 0, 1, row)
         y1 += rows_of(down_in[1], 0, row) - couple * at(h1, 1, 1, row)
+        put(h2, 0, 1, row, x1)
+        put(h2, 1, 1, row, y1)
+        weights = weight(row)
+        keep((HX, 1), row, x1, weights)
+        keep((HY, 1), row, y1, weights)
+        new_x, new_y = electric_xy(e1, h2, 1, row, x1, y1, at(h2, 0, 0, row), at(h2, 1, 0, row))
+        keep((EX, 1), row, new_x, weights)
+        keep((EY, 1), row, new_y, weights)
+        keep((EZ, 1), row, electric_z(e1, h2, 1, row, x1), weights)
+
+    def mix(row):
+        turn_z = minus_x(under, 1, 0, row) - minus_y(at(under, 0, 0, row))
+        put(mixed, 0, 0, row, MAGNETIC * rows_of(up_in[1], 2, row) * turn_z)
+
+    def lower_rows(row):
         couple = MAGNETIC * rows_of(up_in[1], 2, row)
         under_x, under_y = at(under, 0, 0, row), at(under, 1, 0, row)
         under_x += rows_of(up_in[1], 0, row) - couple * under_x - plus_y(at(mixed, 0, 0, row)) - at(s1, 1, 0, row)
         under_y += rows_of(up_in[1], 1, row) - couple * under_y + plus_x(mixed, 0, 0, row) + at(s1, 0, 0, row)
         under_x = jnp.where(has_below, under_x, 0.0)
         under_y = jnp.where(has_below, under_y, 0.0)
-        put(h2, 0, 1, row, x1)
-        put(h2, 1, 1, row, y1)
-        x0, y0 = at(h2, 0, 0, row), at(h2, 1, 0, row)
         weights = weight(row)
-        keep((HX, 1), row, x1, weights)
-        keep((HY, 1), row, y1, weights)
-        for plane, (h_x, h_y, b_x, b_y) in enumerate(((x0, y0, under_x, under_y), (x1, y1, x0, y0))):
-            new_x, new_y = electric_xy(e1, h2, plane, row, h_x, h_y, b_x, b_y)
-            keep((EX, plane), row, new_x, weights)
-            keep((EY, plane), row, new_y, weights)
-        keep((EZ, 1), row, electric_z(e1, h2, 1, row, x1), weights)
-
-    row_tiles(second_rest)
-    send_group(1)
-
-    for group in range(2):
+        new_x, new_y = electric_xy(e1, h2, 0, row, at(h2, 0, 0, row), at(h2, 1, 0, row), under_x, under_y)
+        keep((EX, 0), row, new_x, weights)
+        keep((EY, 0), row, new_y, weights)
+
+    def upper():
+        wait_depth(1, False)
+        row_tiles(upper_rows)
+        send_group(1)
+
+    def lower():
+        wait_depth(1, True)
+        row_tiles(mix)
+        row_tiles(lower_rows)
+        send_group(2)
+
+    def sum_corners(group):
         wait_band(0, group)
         planes_of(group, add_corners)
         send_band(3, group)
 
-    for group in range(2):
+    odd = lax.rem(sub, 2) == 1
+    even = jnp.logical_not(odd)
+    pl.when(odd)(lower)
+    pl.when(even)(upper)
+    sum_corners(0)
+    pl.when(odd)(upper)
+    pl.when(even)(lower)
+
+    @pl.when(odd)
+    def _():
+        sum_corners(2)
+        sum_corners(1)
+
+    @pl.when(even)
+    def _():
+        sum_corners(1)
+        sum_corners(2)
+
+    for group in range(len(GROUPS)):
         wait_band(2, group)
         planes_of(group, add_middle)
         wait_band(1, group)
@@ -528,7 +556,7 @@
 
     for turn in range(2):
         finish_depth(turn)
-    for group in range(2):
+    for group in range(len(GROUPS)):
         for kind in range(4):
             for toward_next in (False, True):
                 band_copy(kind, group, toward_next).wait_send()
@@ -576,8 +604,8 @@
             pltpu.SemaphoreType.DMA((2 * PARTS,)),
             pltpu.SemaphoreType.DMA((2,)),
             pltpu.SemaphoreType.DMA((2,)),
-            pltpu.SemaphoreType.DMA((16,)),
-            pltpu.SemaphoreType.DMA((16,)),
+            pltpu.SemaphoreType.DMA((8 * len(GROUPS),)),
+            pltpu.SemaphoreType.DMA((8 * len(GROUPS),)),
         ],
         compiler_params=pltpu.CompilerParams(
             collective_id=0, has_side_effects=True, vmem_limit_bytes=20 * 2**20),

time: 37.5 us -> 38.9 us (1.037)
  the two profiles are of different devices: /device:TPU:7 before, /device:TPU:128 now
where the time goes in v7:
time: 38.9 us; the launch traced here: 38.8 us
  Pallas kernels  38.8 us (100%)
    pallas_call x1, Pallas kernels, on_device(): pl.pallas_call(functools.partial(kernel, tiles, subs), out_shape=jax.Shap...  37.5 us
    pallas_call x1, Pallas kernels, on_device(): pl.pallas_call(place, out_shape=jax.ShapeDtypeStruct(seeds.shape, f32), i...  1.23 us

profile of v7, /device:TPU:128, one launch (start us, length us, event | category | flops | bytes accessed | tf_op | source)
XLA Modules:
  0.0 38.8 jit_solution(7548611735700836867)
XLA Ops:
  0.0 37.5 %shard_map.46.planes = f32[12,256,128]{2,1,0:T(8,128)S(1)} custom-call(f32[4]{0:T(128)} %decay_in.1, f32[4]{0:T(128)} %coupling_in.1, f32[1,6,2,256,128]{4,3,2,1,0:T(8,128)} %seeds.1, s32[1,2,256,128]{3,2,1,0:T(8,128)} %material.1), custom_call_target="tpu_custom_call" | custom-call | tf_op jit(solution)/shard_map/pallas_call | solution.py:582
  37.5 1.2 %shard_map.47 = f32[1,6,2,256,128]{4,3,2,1,0:T(8,128)} custom-call(f32[12,256,128]{2,1,0:T(8,128)S(1)} %shard_map.46.planes), custom_call_target="tpu_custom_call" | custom-call | tf_op jit(solution)/shard_map/pallas_call | solution.py:613

commit v8 on v6

--- a/solution.py
+++ b/solution.py
@@ -24,6 +24,7 @@
 
 RUN = 8
 PARTS = 3
+LINE = 4
 DIRECT = 104
 PIECES = (((104, 40), (144, 40), (184, 72)), ((104, 72), (176, 40), (216, 40)))
 MOST = 72
@@ -52,7 +53,7 @@
     decay, coupling, field, mat, ca, cb, s0, s1, h1, h2, e1, decayed, under, mixed,
     up_out0, up_out1, down_out0, down_out1, up_in0, up_in1, down_in0, down_in1, relay_in0, relay_in1,
     yc_out, yn_out, xn_out, xc_out, yc_in, yn_in, xn_in, xc_in,
-    load_sem, depth_send, depth_recv, part_send, part_recv, relay_recv, relay_send, band_send, band_recv,
+    load_sem, depth_send, depth_recv, part_send, part_recv, relay_recv, relay_send, band_send, band_recv, word_sem,
 ):
     tile = lax.axis_index("tile")
     sub = lax.axis_index("sub")
@@ -83,8 +84,11 @@
 
     pl.when(has_below)(lambda: greet(tile, below))
     pl.when(has_above)(lambda: greet(tile, above))
-    for other in (x_prev, x_next, y_prev, y_next):
+    in_line = lax.rem(tile, LINE)
+    for other in (y_prev, y_next):
         greet(other, sub)
+    pl.when(in_line > 0)(lambda: greet(x_prev, sub))
+    pl.when(in_line < LINE - 1)(lambda: greet(x_next, sub))
     place_in_run = lax.rem(sub, RUN)
     start = sub - place_in_run
     run_above = start + RUN < subs
@@ -284,8 +288,21 @@
     row_tiles(scale)
     count = lambda flag, number: jnp.where(flag, number, 0)
     crosses_any = jnp.logical_or(crosses_up, crosses_down)
-    pl.semaphore_wait(barrier, 4 + count(has_below, 1) + count(has_above, 1) + count(crosses_any, PARTS))
+    pl.semaphore_wait(barrier, 3 + count(jnp.logical_and(in_line > 0, in_line < LINE - 1), 1) + count(has_below, 1) + count(has_above, 1) + count(crosses_any, PARTS))
+    def pass_word(step):
+        for onward in range(2):
+            place = step if onward else LINE - 1 - step
+
+            @pl.when(in_line == place)
+            def _():
+                if step > 0:
+                    pl.semaphore_wait(word_sem.at[onward], 1)
+                if step < LINE - 1:
+                    pl.semaphore_signal(
+                        word_sem.at[onward], inc=1, device_id=(x_next if onward else x_prev, sub), device_id_type=MESH)
+
     send_depth(0, False)
+    pass_word(0)
     loads[2].wait()
 
     def without_above(hbuf, offset, sbuf, row):
@@ -364,9 +381,11 @@
         decays = rows_of(ca, plane, row)
         return decays * at(ebuf, 2, plane, row) - MAGNETIC * (minus_x(hbuf, 1, plane, row) - minus_y(h_x))
 
+    pass_word(1)
     relay_depth(0, False)
     wait_depth(0)
     relay_depth(1, False)
+    pass_word(2)
 
     def first_rest(row):
         x1 = rows_of(up_out[0], 0, row) - rows_of(down_in[0], 1, row)
@@ -477,6 +496,7 @@
         planes_of(group, pack_middle)
         send_band(2, group)
 
+    pass_word(LINE - 1)
     send_group(0)
     relay_depth(0, True)
     relay_depth(1, True)
@@ -578,6 +598,7 @@
             pltpu.SemaphoreType.DMA((2,)),
             pltpu.SemaphoreType.DMA((16,)),
             pltpu.SemaphoreType.DMA((16,)),
+            pltpu.SemaphoreType.REGULAR((2,)),
         ],
         compiler_params=pltpu.CompilerParams(
             collective_id=0, has_side_effects=True, vmem_limit_bytes=20 * 2**20),

time: 37.5 us -> 39.5 us (1.053)
  the two profiles are of different devices: /device:TPU:7 before, /device:TPU:128 now
where the time goes in v8:
time: 39.5 us; the launch traced here: 39.4 us
  Pallas kernels  39.4 us (100%)
    pallas_call x1, Pallas kernels, on_device(): pl.pallas_call(functools.partial(kernel, tiles, subs), out_shape=jax.Shap...  38.1 us
    pallas_call x1, Pallas kernels, on_device(): pl.pallas_call(place, out_shape=jax.ShapeDtypeStruct(seeds.shape, f32), i...  1.23 us

profile of v8, /device:TPU:128, one launch (start us, length us, event | category | flops | bytes accessed | tf_op | source)
XLA Modules:
  0.0 39.4 jit_solution(3713240816205393212)
XLA Ops:
  0.0 38.1 %shard_map.46.planes = f32[12,256,128]{2,1,0:T(8,128)S(1)} custom-call(f32[4]{0:T(128)} %decay_in.1, f32[4]{0:T(128)} %coupling_in.1, f32[1,6,2,256,128]{4,3,2,1,0:T(8,128)} %seeds.1, s32[1,2,256,128]{3,2,1,0:T(8,128)} %material.1), custom_call_target="tpu_custom_call" | custom-call | tf_op jit(solution)/shard_map/pallas_call | solution.py:574
  38.1 1.2 %shard_map.47 = f32[1,6,2,256,128]{4,3,2,1,0:T(8,128)} custom-call(f32[12,256,128]{2,1,0:T(8,128)S(1)} %shard_map.46.planes), custom_call_target="tpu_custom_call" | custom-call | tf_op jit(solution)/shard_map/pallas_call | solution.py:606

commit v9 on v8

--- a/solution.py
+++ b/solution.py
@@ -74,16 +74,15 @@
         pltpu.make_async_copy(decay_in, decay, load_sem.at[3]),
         pltpu.make_async_copy(coupling_in, coupling, load_sem.at[4]),
     ]
+    barrier = pltpu.get_barrier_semaphore()
+
+    def greet(other_tile, other_sub):
+        pl.semaphore_signal(barrier, inc=1, device_id=(other_tile, other_sub), device_id_type=MESH)
+
+    pl.when(has_below)(lambda: greet(tile, below))
+    pl.when(has_above)(lambda: greet(tile, above))
     for load in loads:
         load.start()
-
-    barrier = pltpu.get_barrier_semaphore()
-
-    def greet(other_tile, other_sub):
-        pl.semaphore_signal(barrier, inc=1, device_id=(other_tile, other_sub), device_id_type=MESH)
-
-    pl.when(has_below)(lambda: greet(tile, below))
-    pl.when(has_above)(lambda: greet(tile, above))
     in_line = lax.rem(tile, LINE)
     for other in (y_prev, y_next):
         greet(other, sub)
@@ -198,7 +197,7 @@
                 part_copy(turn, upward, part).start()
             depth_copy(turn, upward, DIRECT).start()
 
-    late_up = start == 0
+    late_up = start + 2 * RUN < subs
 
     def relay_depth(turn, late):
         for upward in (True, False):
@@ -381,11 +380,11 @@
         decays = rows_of(ca, plane, row)
         return decays * at(ebuf, 2, plane, row) - MAGNETIC * (minus_x(hbuf, 1, plane, row) - minus_y(h_x))
 
-    pass_word(1)
+    for step in range(1, LINE - 1):
+        pass_word(step)
     relay_depth(0, False)
     wait_depth(0)
     relay_depth(1, False)
-    pass_word(2)
 
     def first_rest(row):
         x1 = rows_of(up_out[0], 0, row) - rows_of(down_in[0], 1, row)

time: 39.5 us -> 37.2 us (0.942)
  the two profiles are of different devices: /device:TPU:128 before, /device:TPU:352 now
where the time goes in v9:
time: 37.2 us; the launch traced here: 37 us
  Pallas kernels  37 us (99%)
    pallas_call x1, Pallas kernels, on_device(): pl.pallas_call(functools.partial(kernel, tiles, subs), out_shape=jax.Shap...  35.8 us
    pallas_call x1, Pallas kernels, on_device(): pl.pallas_call(place, out_shape=jax.ShapeDtypeStruct(seeds.shape, f32), i...  1.23 us

profile of v9, /device:TPU:352, one launch (start us, length us, event | category | flops | bytes accessed | tf_op | source)
XLA Modules:
  0.0 37.0 jit_solution(17455215647824733070)
XLA Ops:
  0.0 35.8 %shard_map.46.planes = f32[12,256,128]{2,1,0:T(8,128)S(1)} custom-call(f32[4]{0:T(128)} %decay_in.1, f32[4]{0:T(128)} %coupling_in.1, f32[1,6,2,256,128]{4,3,2,1,0:T(8,128)} %seeds.1, s32[1,2,256,128]{3,2,1,0:T(8,128)} %material.1), custom_call_target="tpu_custom_call" | custom-call | tf_op jit(solution)/shard_map/pallas_call | solution.py:573
  35.8 1.2 %shard_map.47 = f32[1,6,2,256,128]{4,3,2,1,0:T(8,128)} custom-call(f32[12,256,128]{2,1,0:T(8,128)S(1)} %shard_map.46.planes), custom_call_target="tpu_custom_call" | custom-call | tf_op jit(solution)/shard_map/pallas_call | solution.py:605

commit v10 on v9

--- a/solution.py
+++ b/solution.py
@@ -451,46 +451,59 @@
         slot = slot_of(16)
         return jnp.logical_or(slot == 1, slot == 2)
 
-    def pack_corners(index):
-        values = [w[index, first : first + 16, :] for first in corner_rows]
-        low, high = pack_lanes(values)
-        yc_out[0, index], yc_out[1, index] = low, high
+    def corners(index):
+        return [w[index, first : first + 16, :] for first in corner_rows]
+
+    def put_corners(index, values):
+        for first, value in zip(corner_rows, values):
+            w[index, first : first + 16, :] = value
+
+    def swapped(value):
+        return pltpu.roll(value, TY // 2, 1)
+
+    def pack_x(index):
+        values = corners(index)
         middle = middle_lanes()
         for direction in range(2):
-            xn_out[direction, index] = jnp.where(
-                middle, values[2 * direction], pltpu.roll(values[2 * direction + 1], TY // 2, 1))
+            upper, lower = values[2 * direction], swapped(values[2 * direction + 1])
+            xn_out[direction, index] = jnp.where(middle, upper, lower)
+            xc_out[direction, index] = jnp.where(middle, lower, upper)
 
     def pack_middle(index):
         low, high = pack_lanes([w[index, first : first + 48, :] for first in middle_rows])
         yn_out[0, index], yn_out[1, index] = low, high
 
-    def add_corners(index):
+    def add_x_corners(index):
+        values = corners(index)
+        middle = middle_lanes()
+        for side_of in range(2):
+            corner, first = xc_in[side_of, index], 2 - 2 * side_of
+            values[first] += jnp.where(middle, 0.0, corner)
+            values[first + 1] += swapped(jnp.where(middle, corner, 0.0))
+        put_corners(index, values)
+        yc_out[0, index], yc_out[1, index] = pack_lanes(values)
+
+    def add_y_corners(index):
         added = unpack_lanes(yc_in[1, index], yc_in[0, index])
-        values = []
-        for first, more in zip(corner_rows, added):
-            total = w[index, first : first + 16, :] + more
-            w[index, first : first + 16, :] = total
-            values.append(total)
-        middle = middle_lanes()
-        for direction in range(2):
-            xc_out[direction, index] = jnp.where(
-                middle, pltpu.roll(values[2 * direction + 1], TY // 2, 1), values[2 * direction])
+        put_corners(index, [value + more for value, more in zip(corners(index), added)])
 
     def add_middle(index):
         added = unpack_lanes(yn_in[1, index], yn_in[0, index])
         for first, more in zip(middle_rows, added):
             w[index, first : first + 48, :] += more
 
-    def add_x_bands(index):
+    def add_x_middle(index):
+        values = corners(index)
         middle = middle_lanes()
-        for side_of, first in ((1, 0), (0, TX - 32)):
-            plain, summed = xn_in[side_of, index], xc_in[side_of, index]
-            w[index, first : first + 16, :] += jnp.where(middle, plain, summed)
-            w[index, first + 16 : first + 32, :] += pltpu.roll(jnp.where(middle, summed, plain), TY // 2, 1)
+        for side_of in range(2):
+            plain, first = xn_in[side_of, index], 2 - 2 * side_of
+            values[first] += jnp.where(middle, plain, 0.0)
+            values[first + 1] += swapped(jnp.where(middle, 0.0, plain))
+        put_corners(index, values)
 
     def send_group(group):
-        planes_of(group, pack_corners)
-        send_band(0, group)
+        planes_of(group, pack_x)
+        send_band(3, group)
         send_band(1, group)
         planes_of(group, pack_middle)
         send_band(2, group)
@@ -534,16 +547,17 @@
     send_group(1)
 
     for group in range(2):
-        wait_band(0, group)
-        planes_of(group, add_corners)
-        send_band(3, group)
+        wait_band(3, group)
+        planes_of(group, add_x_corners)
+        send_band(0, group)
 
     for group in range(2):
         wait_band(2, group)
         planes_of(group, add_middle)
         wait_band(1, group)
-        wait_band(3, group)
-        planes_of(group, add_x_bands)
+        planes_of(group, add_x_middle)
+        wait_band(0, group)
+        planes_of(group, add_y_corners)
 
     for turn in range(2):
         finish_depth(turn)

time: 37.2 us -> 37.6 us (1.011)
  the two profiles are of different devices: /device:TPU:352 before, /device:TPU:256 now
where the time goes in v10:
time: 37.6 us; the launch traced here: 37.4 us
  Pallas kernels  37.4 us (99%)
    pallas_call x1, Pallas kernels, on_device(): pl.pallas_call(functools.partial(kernel, tiles, subs), out_shape=jax.Shap...  36.2 us
    pallas_call x1, Pallas kernels, on_device(): pl.pallas_call(place, out_shape=jax.ShapeDtypeStruct(seeds.shape, f32), i...  1.23 us

profile of v10, /device:TPU:256, one launch (start us, length us, event | category | flops | bytes accessed | tf_op | source)
XLA Modules:
  0.0 37.4 jit_solution(362751359359955606)
XLA Ops:
  0.0 36.2 %shard_map.46.planes = f32[12,256,128]{2,1,0:T(8,128)S(1)} custom-call(f32[4]{0:T(128)} %decay_in.1, f32[4]{0:T(128)} %coupling_in.1, f32[1,6,2,256,128]{4,3,2,1,0:T(8,128)} %seeds.1, s32[1,2,256,128]{3,2,1,0:T(8,128)} %material.1), custom_call_target="tpu_custom_call" | custom-call | tf_op jit(solution)/shard_map/pallas_call | solution.py:587
  36.2 1.2 %shard_map.47 = f32[1,6,2,256,128]{4,3,2,1,0:T(8,128)} custom-call(f32[12,256,128]{2,1,0:T(8,128)S(1)} %shard_map.46.planes), custom_call_target="tpu_custom_call" | custom-call | tf_op jit(solution)/shard_map/pallas_call | solution.py:619

commit v11 on v9

--- a/solution.py
+++ b/solution.py
@@ -25,8 +25,8 @@
 RUN = 8
 PARTS = 3
 LINE = 4
-DIRECT = 104
-PIECES = (((104, 40), (144, 40), (184, 72)), ((104, 72), (176, 40), (216, 40)))
+DIRECT = (104, 88)
+PIECES = (((104, 40), (144, 40), (184, 72)), ((88, 64), (152, 56), (208, 48)))
 MOST = 72
 
 
@@ -195,7 +195,7 @@
         def _():
             for part in (1, 0, 2) if not upward else (1, 2, 0):
                 part_copy(turn, upward, part).start()
-            depth_copy(turn, upward, DIRECT).start()
+            depth_copy(turn, upward, DIRECT[int(upward)]).start()
 
     late_up = start + 2 * RUN < subs
 
@@ -220,7 +220,7 @@
 
             @pl.when(crosses)
             def _():
-                depth_copy(turn, upward, DIRECT).wait_recv()
+                depth_copy(turn, upward, DIRECT[int(upward)]).wait_recv()
                 for part in range(PARTS):
                     relay_copy(turn, upward, part).wait_recv()
 
@@ -233,7 +233,7 @@
             def _():
                 for part in range(PARTS):
                     part_copy(turn, upward, part).wait_send()
-                depth_copy(turn, upward, DIRECT).wait_send()
+                depth_copy(turn, upward, DIRECT[int(upward)]).wait_send()
 
             for part in range(PARTS):
                 pl.when(relays(upward, part))(lambda: relay_copy(turn, upward, part).wait_send())

time: 37.2 us -> 36.2 us (0.973)
  the two profiles are of different devices: /device:TPU:352 before, /device:TPU:7 now
where the time goes in v11:
time: 36.2 us; the launch traced here: 36.1 us
  Pallas kernels  36.1 us (100%)
    pallas_call x1, Pallas kernels, on_device(): pl.pallas_call(functools.partial(kernel, tiles, subs), out_shape=jax.Shap...  34.9 us
    pallas_call x1, Pallas kernels, on_device(): pl.pallas_call(place, out_shape=jax.ShapeDtypeStruct(seeds.shape, f32), i...  1.23 us

profile of v11, /device:TPU:7, one launch (start us, length us, event | category | flops | bytes accessed | tf_op | source)
XLA Modules:
  0.0 36.1 jit_solution(15911978809263145485)
XLA Ops:
  0.0 34.9 %shard_map.46.planes = f32[12,256,128]{2,1,0:T(8,128)S(1)} custom-call(f32[4]{0:T(128)} %decay_in.1, f32[4]{0:T(128)} %coupling_in.1, f32[1,6,2,256,128]{4,3,2,1,0:T(8,128)} %seeds.1, s32[1,2,256,128]{3,2,1,0:T(8,128)} %material.1), custom_call_target="tpu_custom_call" | custom-call | tf_op jit(solution)/shard_map/pallas_call | solution.py:573
  34.9 1.2 %shard_map.47 = f32[1,6,2,256,128]{4,3,2,1,0:T(8,128)} custom-call(f32[12,256,128]{2,1,0:T(8,128)S(1)} %shard_map.46.planes), custom_call_target="tpu_custom_call" | custom-call | tf_op jit(solution)/shard_map/pallas_call | solution.py:605

commit v12 on v11

--- a/solution.py
+++ b/solution.py
@@ -21,6 +21,7 @@
 LATE = ((HX, 1), (HY, 1), (EX, 0), (EY, 0), (EX, 1), (EY, 1), (EZ, 1))
 ORDER = EARLY + LATE
 GROUPS = ((0, len(EARLY)), (len(EARLY), len(LATE)))
+PLACE = tuple(2 * comp + plane for comp, plane in ORDER)
 
 RUN = 8
 PARTS = 3
@@ -40,12 +41,8 @@
 
 def planes_of(group, body):
     first, count = GROUPS[group]
-
-    def step(index, carry):
+    for index in range(first, first + count):
         body(index)
-        return carry
-
-    lax.fori_loop(first, first + count, step, 0, unroll=True)
 
 
 def kernel(
@@ -406,7 +403,7 @@
     row_tiles(first_rest)
 
     def keep(name, row, value, weights):
-        w[ORDER.index(name), pl.ds(row, ROWS), :] = value * weights
+        w[2 * name[0] + name[1], pl.ds(row, ROWS), :] = value * weights
 
     def second_local(row):
         new_x, new_y, new_z, new_z1 = magnetic_local(h1, 0, s1, row)
@@ -452,7 +449,7 @@
         return jnp.logical_or(slot == 1, slot == 2)
 
     def pack_corners(index):
-        values = [w[index, first : first + 16, :] for first in corner_rows]
+        values = [w[PLACE[index], first : first + 16, :] for first in corner_rows]
         low, high = pack_lanes(values)
         yc_out[0, index], yc_out[1, index] = low, high
         middle = middle_lanes()
@@ -461,15 +458,15 @@
                 middle, values[2 * direction], pltpu.roll(values[2 * direction + 1], TY // 2, 1))
 
     def pack_middle(index):
-        low, high = pack_lanes([w[index, first : first + 48, :] for first in middle_rows])
+        low, high = pack_lanes([w[PLACE[index], first : first + 48, :] for first in middle_rows])
         yn_out[0, index], yn_out[1, index] = low, high
 
     def add_corners(index):
         added = unpack_lanes(yc_in[1, index], yc_in[0, index])
         values = []
         for first, more in zip(corner_rows, added):
-            total = w[index, first : first + 16, :] + more
-            w[index, first : first + 16, :] = total
+            total = w[PLACE[index], first : first + 16, :] + more
+            w[PLACE[index], first : first + 16, :] = total
             values.append(total)
         middle = middle_lanes()
         for direction in range(2):
@@ -479,14 +476,14 @@
     def add_middle(index):
         added = unpack_lanes(yn_in[1, index], yn_in[0, index])
         for first, more in zip(middle_rows, added):
-            w[index, first : first + 48, :] += more
+            w[PLACE[index], first : first + 48, :] += more
 
     def add_x_bands(index):
         middle = middle_lanes()
         for side_of, first in ((1, 0), (0, TX - 32)):
             plain, summed = xn_in[side_of, index], xc_in[side_of, index]
-            w[index, first : first + 16, :] += jnp.where(middle, plain, summed)
-            w[index, first + 16 : first + 32, :] += pltpu.roll(jnp.where(middle, summed, plain), TY // 2, 1)
+            w[PLACE[index], first : first + 16, :] += jnp.where(middle, plain, summed)
+            w[PLACE[index], first + 16 : first + 32, :] += pltpu.roll(jnp.where(middle, summed, plain), TY // 2, 1)
 
     def send_group(group):
         planes_of(group, pack_corners)
@@ -551,17 +548,6 @@
         for kind in range(4):
             for toward_next in (False, True):
                 band_copy(kind, group, toward_next).wait_send()
-
-
-def place(planes, out, sems):
-    copies = [
-        pltpu.make_async_copy(planes.at[index], out.at[0, comp, plane], sems.at[index])
-        for index, (comp, plane) in enumerate(ORDER)
-    ]
-    for copy in copies:
-        copy.start()
-    for copy in copies:
-        copy.wait()
 
 
 def on_device(tiles, subs, seeds, material, decay, coupling):
@@ -602,14 +588,7 @@
         compiler_params=pltpu.CompilerParams(
             collective_id=0, has_side_effects=True, vmem_limit_bytes=20 * 2**20),
     )(*(pltpu.with_memory_space_constraint(array, pltpu.HBM) for array in (decay, coupling, seeds, material)))
-    return pl.pallas_call(
-        place,
-        out_shape=jax.ShapeDtypeStruct(seeds.shape, f32),
-        in_specs=[pl.BlockSpec(memory_space=pltpu.VMEM)],
-        out_specs=hbm,
-        scratch_shapes=[pltpu.SemaphoreType.DMA((planes,))],
-        compiler_params=pltpu.CompilerParams(vmem_limit_bytes=4 * 2**20),
-    )(done)
+    return done.reshape(seeds.shape)
 
 
 def solution(mesh):

time: 36.2 us -> 36.1 us (level)
  Pallas kernels: 36.1 us -> 34.9 us
  local copies, waits for them, and re-layouts: 0 us -> 1.15 us
    pallas_call x1 -> x0, Pallas kernels: 1.23 us -> none  [on_device(): pl.pallas_call(place, out_shape=jax.ShapeDtypeStruct(seeds.shape, f32), i...]
    unnamed x0 -> x1, local copies, waits for them, and re-layouts: none -> 1.15 us
where the time goes in v12:
time: 36.1 us; the launch traced here: 36 us
  Pallas kernels  34.9 us (97%)
  local copies, waits for them, and re-layouts  1.15 us (3%)
    pallas_call x1, Pallas kernels, on_device(): pl.pallas_call(functools.partial(kernel, tiles, subs), out_shape=jax.Shap...  34.9 us
    unnamed x1, local copies, waits for them, and re-layouts  1.15 us

profile of v12, /device:TPU:7, one launch (start us, length us, event | category | flops | bytes accessed | tf_op | source)
XLA Modules:
  0.0 36.0 jit_solution(2906813382654377585)
XLA Ops:
  0.0 34.9 %shard_map.46 = f32[12,256,128]{2,1,0:T(8,128)S(1)} custom-call(f32[4]{0:T(128)} %decay_in.1, f32[4]{0:T(128)} %coupling_in.1, f32[1,6,2,256,128]{4,3,2,1,0:T(8,128)} %seeds.1, s32[1,2,256,128]{3,2,1,0:T(8,128)} %material.1), custom_call_target="tpu_custom_call" | custom-call | tf_op jit(solution)/shard_map/pallas_call | solution.py:559
  34.9 1.1 %copy.6 = f32[1,6,2,256,128]{4,3,2,1,0:T(8,128)} copy(f32[1,6,2,256,128]{4,3,2,1,0:T(8,128)S(1)} %bitcast.1) | data formatting | bytes 3145728

commit v13 on v12

--- a/solution.py
+++ b/solution.py
@@ -36,7 +36,7 @@
         body(pl.multiple_of(index * ROWS, ROWS))
         return carry
 
-    lax.fori_loop(0, TX // ROWS, step, 0, unroll=2)
+    lax.fori_loop(0, TX // ROWS, step, 0, unroll=4)
 
 
 def planes_of(group, body):

time: 36.1 us -> 35.9 us (level)
  no operation moved by 1% of the time
where the time goes in v13:
time: 35.9 us; the launch traced here: 35.7 us
  Pallas kernels  34.6 us (96%)
  local copies, waits for them, and re-layouts  1.15 us (3%)
    pallas_call x1, Pallas kernels, on_device(): pl.pallas_call(functools.partial(kernel, tiles, subs), out_shape=jax.Shap...  34.6 us
    unnamed x1, local copies, waits for them, and re-layouts  1.15 us

profile of v13, /device:TPU:7, one launch (start us, length us, event | category | flops | bytes accessed | tf_op | source)
XLA Modules:
  0.0 35.7 jit_solution(13947268945187052183)
XLA Ops:
  0.0 34.6 %shard_map.46 = f32[12,256,128]{2,1,0:T(8,128)S(1)} custom-call(f32[4]{0:T(128)} %decay_in.1, f32[4]{0:T(128)} %coupling_in.1, f32[1,6,2,256,128]{4,3,2,1,0:T(8,128)} %seeds.1, s32[1,2,256,128]{3,2,1,0:T(8,128)} %material.1), custom_call_target="tpu_custom_call" | custom-call | tf_op jit(solution)/shard_map/pallas_call | solution.py:559
  34.6 1.1 %copy.6 = f32[1,6,2,256,128]{4,3,2,1,0:T(8,128)} copy(f32[1,6,2,256,128]{4,3,2,1,0:T(8,128)S(1)} %bitcast.1) | data formatting | bytes 3145728

commit v14 on v13

--- a/solution.py
+++ b/solution.py
@@ -36,7 +36,7 @@
         body(pl.multiple_of(index * ROWS, ROWS))
         return carry
 
-    lax.fori_loop(0, TX // ROWS, step, 0, unroll=4)
+    lax.fori_loop(0, TX // ROWS, step, 0, unroll=8)
 
 
 def planes_of(group, body):

time: 35.9 us -> 35.9 us (level)
  no operation moved by 1% of the time
where the time goes in v14:
time: 35.9 us; the launch traced here: 35.7 us
  Pallas kernels  34.6 us (96%)
  local copies, waits for them, and re-layouts  1.15 us (3%)
    pallas_call x1, Pallas kernels, on_device(): pl.pallas_call(functools.partial(kernel, tiles, subs), out_shape=jax.Shap...  34.6 us
    unnamed x1, local copies, waits for them, and re-layouts  1.15 us

profile of v14, /device:TPU:7, one launch (start us, length us, event | category | flops | bytes accessed | tf_op | source)
XLA Modules:
  0.0 35.7 jit_solution(17198864280490783659)
XLA Ops:
  0.0 34.6 %shard_map.46 = f32[12,256,128]{2,1,0:T(8,128)S(1)} custom-call(f32[4]{0:T(128)} %decay_in.1, f32[4]{0:T(128)} %coupling_in.1, f32[1,6,2,256,128]{4,3,2,1,0:T(8,128)} %seeds.1, s32[1,2,256,128]{3,2,1,0:T(8,128)} %material.1), custom_call_target="tpu_custom_call" | custom-call | tf_op jit(solution)/shard_map/pallas_call | solution.py:559
  34.6 1.1 %copy.6 = f32[1,6,2,256,128]{4,3,2,1,0:T(8,128)} copy(f32[1,6,2,256,128]{4,3,2,1,0:T(8,128)S(1)} %bitcast.1) | data formatting | bytes 3145728
